TPU v7x, 256 devices: a whole 4x4x8 slice. The times are simulated.
256 devices in a mesh: diff: 128 (over z, x, y_hi, core), obj: 2 (over y_lo).
Axes of the slice: x: 4, y: 4 (y_hi: 2, y_lo: 2; y = y_hi * 2 + y_lo), z: 8, core: 2. Of those that a mesh axis runs over, the one named last changes fastest.
Arguments:
- object_field: float32 [2, 32768, 512], P(None, ('diff', 'obj')), may hold values from -6 to 6
- probe_modes: float32 [4, 2, 256, 256], P('obj'), may hold values from -3 to 3
- amplitudes: float32 [256, 256, 256], P('diff')
- offsets: int32 [256, 2], P('diff'), may hold values from 0 to 256, as said below
- counts: int32 [128], replicated, may hold values from 1 to 2, as said below
Outputs:
- object_out: float32 [2, 32768, 512], P(None, ('diff', 'obj'))
- probe_out: float32 [4, 2, 256, 256], P('obj')
Inputs may be any that keep to these rules, and one draw needn't show every extreme that they name: Row k of offsets holds the block-local corner of slot k (block k // 2): offsets[k,0] < 256, and offsets[k,0] <= 0 in the last block; offsets[k,1] <= 256. Every slot, used or not, holds such a corner. Block b uses its first counts[b] slots.
All inputs are finite; a program needn't handle non-finite values.
Results may differ from a plain program's by a relative error of at most 0.0003.
Values sent between devices are 32-bit elements; how exact they have to be, the bound alone decides.
No kernel may reach another device: no remote copies, remote signals or barrier semaphores. Data moves between devices by JAX's collectives and lax.ppermute only.
A program may use at most 64 MiB of HBM per device.

v0:
```python
import jax
import jax.numpy as jnp
from jax import lax
from jax.sharding import PartitionSpec as P

PASSES = 3


EDGE_SCALE = 1.0
DIFFUSION_RATE = 0.2
OBJECT_STEP = 0.25
HIGHEST = lax.Precision.HIGHEST


def passed_along(value, axis, steps):
    count = lax.axis_size(axis)
    initial, last = (max(0, -steps), min(count, count - steps))
    return lax.ppermute(value, axis, [(source, source + steps) for source in range(initial, last)])


def extended_2(block, sides, width):
    for axis, dim in sides:
        count = lax.axis_size(axis)
        forward = [(i, i + 1) for i in range(count - 1)]
        backward = [(target, source) for source, target in forward]
        low = lax.ppermute(
            lax.slice_in_dim(block, block.shape[dim] - width, None, axis=dim), axis, forward
        )
        high = lax.ppermute(lax.slice_in_dim(block, 0, width, axis=dim), axis, backward)
        block = jnp.concatenate([low, block, high], axis=dim)
    return block


def dft_tables(length):
    ladder = jnp.arange(length, dtype=jnp.int32)
    product = ladder[:, None] * ladder[None, :] % length
    angle = product.astype(jnp.float32) * (2.0 * jnp.pi / length)
    scaling = 1.0 / jnp.sqrt(jnp.float32(length))
    return (jnp.cos(angle) * scaling, jnp.sin(angle) * scaling)


def apply_left(table, stacked):
    return jnp.einsum("jk,mkl->mjl", table, stacked, precision=HIGHEST)


def apply_right(stacked, table):
    return jnp.einsum("mjk,kl->mjl", stacked, table, precision=HIGHEST)


def to_detector(real_part, imag_part, cosine, sine_table):
    mid_real = apply_left(cosine, real_part) + apply_left(sine_table, imag_part)
    mid_imag = apply_left(cosine, imag_part) - apply_left(sine_table, real_part)
    out_real = apply_right(mid_real, cosine) + apply_right(mid_imag, sine_table)
    out_imag = apply_right(mid_imag, cosine) - apply_right(mid_real, sine_table)
    return (out_real, out_imag)


def to_sample(real_part, imag_part, cosine, sine_table):
    mid_real = apply_left(cosine, real_part) - apply_left(sine_table, imag_part)
    mid_imag = apply_left(cosine, imag_part) + apply_left(sine_table, real_part)
    out_real = apply_right(mid_real, cosine) - apply_right(mid_imag, sine_table)
    out_imag = apply_right(mid_imag, cosine) + apply_right(mid_real, sine_table)
    return (out_real, out_imag)


def detector_waves(patch_field, probe_modes, cosine, sine_table):
    probe_real = probe_modes[:, 0]
    probe_imag = probe_modes[:, 1]
    wave_real = probe_real * patch_field[0] - probe_imag * patch_field[1]
    wave_imag = probe_real * patch_field[1] + probe_imag * patch_field[0]
    far_real, far_imag = to_detector(wave_real, wave_imag, cosine, sine_table)
    return (far_real, far_imag, jnp.sum(far_real * far_real + far_imag * far_imag, axis=0))


def gradients(patch_field, probe_modes, far_real, far_imag, power, amplitude, cosine, sine_table):
    factor = amplitude / jnp.sqrt(power + 1.0) - 1.0
    back_real, back_imag = to_sample(far_real * factor, far_imag * factor, cosine, sine_table)
    probe_real = probe_modes[:, 0]
    probe_imag = probe_modes[:, 1]
    patch_grad = jnp.stack(
        [
            jnp.sum(probe_real * back_real + probe_imag * back_imag, axis=0),
            jnp.sum(probe_real * back_imag - probe_imag * back_real, axis=0),
        ]
    )
    probe_grad = jnp.stack(
        [
            patch_field[0] * back_real + patch_field[1] * back_imag,
            patch_field[0] * back_imag - patch_field[1] * back_real,
        ],
        axis=1,
    )
    return (patch_grad, probe_grad)


def edge_flux(difference):
    weight = 1.0 / (
        1.0 + jnp.sum(difference * difference, axis=0, keepdims=True) / (EDGE_SCALE * EDGE_SCALE)
    )
    return difference * weight


def diffuse(stacked, row_ids, total_rows):
    center = stacked[:, 1:-1]
    inner_ids = row_ids[1:-1]
    valid_up = ((inner_ids >= 1) & (inner_ids <= total_rows)).astype(stacked.dtype)
    valid_down = ((inner_ids >= -1) & (inner_ids < total_rows - 1)).astype(stacked.dtype)
    upward = edge_flux(stacked[:, :-2] - center) * valid_up[None, :, None]
    downward = edge_flux(stacked[:, 2:] - center) * valid_down[None, :, None]
    across = edge_flux(center[:, :, 1:] - center[:, :, :-1])
    zero_column = jnp.zeros_like(center[:, :, :1])
    sideways = jnp.concatenate([across, zero_column], axis=2) - jnp.concatenate(
        [zero_column, across], axis=2
    )
    return center + DIFFUSION_RATE * (upward + downward + sideways)


def pick(array, position):
    return lax.dynamic_index_in_dim(array, position, 0, keepdims=False)


def add_patch(grand, piece, corner, weight):
    anchor = (jnp.int32(0), corner[0], corner[1])
    current = lax.dynamic_slice(grand, anchor, piece.shape)
    return lax.dynamic_update_slice(grand, current + weight * piece, anchor)


def body(object_field, probe_modes, amplitudes, offsets, counts):
    tile_rows = object_field.shape[1]
    columns = object_field.shape[2]
    length = probe_modes.shape[-1]
    slots = amplitudes.shape[0]
    n_obj = lax.axis_size("obj")
    n_diff = lax.axis_size("diff")
    block_rows = tile_rows * n_obj
    total_rows = block_rows * n_diff
    diff_rank = lax.axis_index("diff")
    start_row = (diff_rank * n_obj + lax.axis_index("obj")) * tile_rows
    cosine, sine_table = dft_tables(length)
    own_count = pick(counts, diff_rank)
    block = lax.all_gather(object_field, "obj", axis=1, tiled=True)
    following = passed_along(block, "diff", -1)
    extended = jnp.concatenate([block, following], axis=1)
    probe_now = probe_modes

    def cut(slot):
        corner = pick(offsets, slot)
        return lax.dynamic_slice(
            extended, (jnp.int32(0), corner[0], corner[1]), (2, length, length)
        )

    def work(patch_field, amplitude):
        far_real, far_imag, partial_power = detector_waves(
            patch_field, probe_now, cosine, sine_table
        )
        power = lax.psum(partial_power, "obj")
        return gradients(
            patch_field, probe_now, far_real, far_imag, power, amplitude, cosine, sine_table
        )

    zero_grad = jnp.zeros((2, 2 * block_rows, columns), jnp.float32)
    zero_probe = jnp.zeros_like(probe_now)

    def own_step(slot, carry):
        grand, probe_sum = carry
        weight = (slot < own_count).astype(jnp.float32)
        patch_grad, probe_grad = work(cut(slot), pick(amplitudes, slot))
        grand = add_patch(grand, patch_grad, pick(offsets, slot), weight)
        return (grand, probe_sum + weight * probe_grad)

    grad_ext, probe_grad_sum = lax.fori_loop(0, slots, own_step, (zero_grad, zero_probe))
    spilled = passed_along(grad_ext[:, block_rows:], "diff", 1)
    tile_grad = lax.psum_scatter(
        grad_ext[:, :block_rows] + spilled, "obj", scatter_dimension=1, tiled=True
    )
    probe_total = lax.psum(probe_grad_sum, "diff")
    raised = object_field + OBJECT_STEP * tile_grad
    smooth = raised
    row_ids = start_row + jnp.arange(-1, tile_rows + 1, dtype=jnp.int32)
    for sweep in range(PASSES):
        margin = extended_2(smooth, ((("diff", "obj"), 1),), 1)
        smooth = diffuse(margin, row_ids, total_rows)
    probe_modes = probe_now + probe_total / n_diff
    return (smooth, probe_modes)


def solution(mesh):
    placed = (
        P(None, ("diff", "obj"), None),
        P("obj", None, None, None),
        P("diff", None, None),
        P("diff", None),
        P(),
    )
    return jax.shard_map(
        body,
        mesh=mesh,
        in_specs=placed,
        out_specs=(P(None, ("diff", "obj"), None), P("obj", None, None, None)),
        check_vma=False,
    )
```

profile of v0, /device:TPU:128, one launch (start us, length us, event | category | flops | bytes accessed | tf_op | source)
XLA Modules:
  0.0 1596.2 jit_solution(2347313864426878578)
XLA Ops:
  7.9 29.8 %all-gather.2.cloned.1.call-done = f32[2,256,512]{2,1,0:T(8,128)} async-done(((f32[2,128,512]{2,1,0:T(8,128)}), f32[2,256,512]{2,1,0:T(8,128)}) %all-gather.2.cloned.1.call-update) | async-done | bytes 1048592 | tf_op jit(solution)/shard_map/all_gather | solution.py:141
  37.7 6.1 collective-permute-start
  45.7 10.7 collective-permute-done
  59.5 171.4 %while.19 = (s32[]{:T(128)}, f32[2,512,512]{2,1,0:T(8,128)}, f32[2,2,256,256]{3,2,0,1:T(8,128)}, s32[2,2]{1,0:T(2,128)S(1)}, s32[]{:T(128)}, /*index=5*/f32[2,2,...) while((s32[]{:T(128)}, f32[2,512,512]{2,1,0:T(8,128)}, ...), condition=%wide.region_5.6_spmd.clone.clone, body=%wide.region_0.5_spmd.clone.clone.sunk | while | flops 6465191936 | bytes 39321936 | solution.py:171
  65.2 1.9 fusion.241
  67.1 1.9 fusion.238
  69.0 1.9 fusion.242
  72.7 1.9 fusion.239
  76.4 1.8 convolution_add_fusion.6
  78.3 2.5 add_reduce_fusion.2
  81.4 36.9 %all-reduce.11.cloned.1.call-done = f32[256,256]{1,0:T(8,128)} async-done(((f32[256,256]{1,0:T(8,128)}), f32[256,256]{1,0:T(8,128)}) %all-reduce.11.cloned.1.call-update) | async-done | bytes 262160 | tf_op jit(solution)/shard_map/while/body/eval_jaxpr/psum | solution.py:156
  123.0 1.9 fusion.249
  124.9 1.9 fusion.246
  126.8 1.8 fusion.247
  128.6 1.8 fusion.250
  130.5 1.9 convolution_add_fusion.7
  132.3 2.0 add_bitcast_fusion.2
  135.7 6.2 dynamic_update_slice.13
  148.8 1.9 fusion.241
  150.7 1.9 fusion.238
  152.6 1.9 fusion.242
  156.3 1.9 fusion.239
  161.9 2.5 add_reduce_fusion.2
  165.0 35.9 %all-reduce.11.cloned.1.call-done = f32[256,256]{1,0:T(8,128)} async-done(((f32[256,256]{1,0:T(8,128)}), f32[256,256]{1,0:T(8,128)}) %all-reduce.11.cloned.1.call-update) | async-done | bytes 262160 | tf_op jit(solution)/shard_map/while/body/eval_jaxpr/psum | solution.py:156
  205.6 1.9 fusion.249
  207.4 1.9 fusion.246
  209.3 1.8 fusion.247
  211.1 1.8 fusion.250
  213.0 1.9 convolution_add_fusion.7
  214.8 2.0 add_bitcast_fusion.2
  218.3 6.5 dynamic_update_slice.13
  224.7 2.3 fusion.252
  230.9 2.4 slice.144
  233.3 2.0 collective-permute-start.1
  236.5 19.2 %collective-permute-done.1 = f32[2,256,512]{2,1,0:T(8,128)} collective-permute-done((f32[2,256,512]{2,1,0:T(8,128)}, f32[2,256,512]{2,1,0:T(8,128)}, u32[]{:S(2)}, u32[]{:S(2)}) %collective-permute-start.1) | collective-permute-done | bytes 1048608 | tf_op jit(solution)/shard_map/ppermute | solution.py:18
  255.7 2.4 slice_add_fusion
  258.2 1261.3 %all-reduce.9.cloned.1.call-done = f32[2,2,256,256]{3,2,1,0:T(8,128)} async-done(((f32[2,2,256,256]{3,2,1,0:T(8,128)}), f32[2,2,256,256]{3,2,1,0:T(8,128)}) %all-reduce.9.cloned.1.call-update) | async-done | bytes 1048592 | tf_op jit(solution)/shard_map/psum | solution.py:176
  1519.5 2.3 multiply_add_fusion
  1521.8 22.7 %reduce-scatter.2.cloned.1.call-done = f32[2,128,512]{2,1,0:T(8,128)} async-done(((f32[2,256,512]{2,1,0:T(8,128)}), f32[2,128,512]{2,1,0:T(8,128)}) %reduce-scatter.2.cloned.1.call-update) | async-done | bytes 524304 | tf_op jit(solution)/shard_map/reduce_scatter | solution.py:173
  1545.9 5.3 collective-permute-start.3
  1551.2 1.9 collective-permute-start.2
  1553.4 8.2 collective-permute-done.2
  1562.4 1.9 collective-permute-start.5
  1564.3 3.9 collective-permute-start.4
  1568.5 6.2 collective-permute-done.4
  1575.6 1.9 collective-permute-start.7
  1577.5 3.9 collective-permute-start.6
  1581.7 6.2 collective-permute-done.6
  (81 shorter events, 38.4 us)
Async XLA Ops:
  7.2 37.9 %copy-start.7 = (s32[128]{0:T(128)S(1)}, s32[128]{0:T(128)}, u32[]{:S(2)}) copy-start(s32[128]{0:T(128)} %param.11) | copy-start | bytes 1540
  7.2 30.5 %all-gather.2.cloned.1.call-start = ((), (), s32[]{:S(2)}) async-start(), calls=%async_computation.1 | async-start | bytes 1572864 | tf_op jit(solution)/shard_map/all_gather | solution.py:141
  37.7 18.7 %copy-start.5 = (f32[2,256,512]{2,1,0:T(8,128)S(1)}, f32[2,256,512]{2,1,0:T(8,128)}, u32[]{:S(2)}) copy-start(f32[2,256,512]{2,1,0:T(8,128)} %all-gather.2.cloned.1.call-done) | copy-start | bytes 3145732
  37.7 18.7 %collective-permute-start = (f32[2,256,512]{2,1,0:T(8,128)}, f32[2,256,512]{2,1,0:T(8,128)S(1)}, u32[]{:S(2)}, u32[]{:S(2)}) collective-permute-start(f32[2,256,512]{2,1,0:T(8,128)} %all-gather.2.cloned.1.call-done), channel_id=1, source_target_pairs={{2,0},{4,2},{6,4},{8,6},{10,8},{12,10},{14,12},{16,14},{18,16},{20... | collective-permute-start | bytes 3145736 | tf_op jit(solution)/shard_map/ppermute | solution.py:18
  57.9 1.6 copy-start.3
  57.9 1.6 copy-start.6
  59.5 58.9 %all-reduce.11.cloned.1.call-start = ((), (), s32[]{:S(2)}) async-start(), calls=%async_computation.4 | async-start | bytes 524288 | tf_op jit(solution)/shard_map/while/body/eval_jaxpr/psum | solution.py:156
  143.1 57.8 %all-reduce.11.cloned.1.call-start = ((), (), s32[]{:S(2)}) async-start(), calls=%async_computation.4 | async-start | bytes 524288 | tf_op jit(solution)/shard_map/while/body/eval_jaxpr/psum | solution.py:156
  230.9 4.5 copy-start
  230.9 1288.6 %all-reduce.9.cloned.1.call-start = ((), (), s32[]{:S(2)}) async-start(), calls=%async_computation.3 | async-start | bytes 2097152 | tf_op jit(solution)/shard_map/psum | solution.py:176
  233.3 22.4 %copy-start.1 = (f32[2,512,512]{2,1,0:T(8,128)S(1)}, f32[2,512,512]{2,1,0:T(8,128)}, u32[]{:S(2)}) copy-start(f32[2,512,512]{2,1,0:T(8,128)} %get-tuple-element.287) | copy-start | bytes 6291460
  233.3 22.4 %collective-permute-start.1 = (f32[2,256,512]{2,1,0:T(8,128)}, f32[2,256,512]{2,1,0:T(8,128)}, u32[]{:S(2)}, u32[]{:S(2)}) collective-permute-start(f32[2,256,512]{2,1,0:T(8,128)} %slice.144), channel_id=1, source_target_pairs={{0,2},{2,4},{4,6},{6,8},{8,10},{10,12},{12,14},{14,16},{16,18},{18... | collective-permute-start | bytes 3145736 | tf_op jit(solution)/shard_map/ppermute | solution.py:18
  236.4 1283.1 %copy-start.2 = (f32[2,2,256,256]{3,2,1,0:T(8,128)S(1)}, f32[2,2,256,256]{3,2,1,0:T(8,128)}, u32[]{:S(2)}) copy-start(f32[2,2,256,256]{3,2,1,0:T(8,128)} %param.8) | copy-start | bytes 3145732
  236.4 1308.1 %reduce-scatter.2.cloned.1.call-start = ((), (), s32[]{:S(2)}) async-start(), calls=%async_computation.2 | async-start | bytes 1572864 | tf_op jit(solution)/shard_map/reduce_scatter | solution.py:173
  258.1 1286.4 %copy-start.4 = (f32[2,128,512]{2,1,0:T(8,128)S(1)}, f32[2,128,512]{2,1,0:T(8,128)}, u32[]{:S(2)}) copy-start(f32[2,128,512]{2,1,0:T(8,128)} %param.7) | copy-start | bytes 1572868
  1545.9 7.5 collective-permute-start.3
  1551.2 10.4 collective-permute-start.2
  1562.4 6.1 collective-permute-start.5
  1564.3 10.4 collective-permute-start.4
  1575.6 6.1 collective-permute-start.7
  1577.5 10.4 collective-permute-start.6
Sparse Core Ops, SparseCore 0:
  9.8 27.8 all-gather.1
  81.0 37.3 all-reduce.10
  164.6 36.2 all-reduce.10
  236.5 1282.9 all-reduce.8
  1521.8 22.6 reduce-scatter.1
where the time goes:
time: 1620 us; the launch traced here: 1600 us
  waiting for transfers between devices  1440 us (89%)
  matrix products  61 us (4%)
  starting transfers between devices  27.1 us (2%)
  local copies, waits for them, and re-layouts  23.4 us (1%)
  other arithmetic  19.7 us (1%)
    psum x1, waiting for transfers between devices, body(): probe_total = lax.psum(probe_grad_sum, 'diff')  1260 us
    psum x2, waiting for transfers between devices, work(): power = lax.psum(partial_power, 'obj')  72.8 us
  transfers between devices with their start and end apart: 13, of which 10 were waited for; matrix products, arithmetic and copies ran while one was open for 1% of the time, Pallas kernels for 0%

commit v1 on v0

v1 whole, which is shorter than its diff:
```python
import functools

import jax
import jax.numpy as jnp
import numpy as np
from jax import lax
from jax.experimental import pallas as pl
from jax.experimental.pallas import tpu as pltpu
from jax.sharding import Mesh
from jax.sharding import PartitionSpec as P


PASSES = 3
EDGE_SCALE = 1.0
DIFFUSION_RATE = 0.2
OBJECT_STEP = 0.25
HALO = 8
INTERPRET = False
F32 = jnp.float32
BF16 = jnp.bfloat16
DIFF = ("chip", "core")
VMEM = pl.BlockSpec(memory_space=pltpu.VMEM)
SMEM = pl.BlockSpec(memory_space=pltpu.SMEM)


def call(kernel, out_shape, in_specs, scratch=(), mib=8):
    single = not isinstance(out_shape, (tuple, list))
    return pl.pallas_call(
        kernel,
        out_shape=out_shape,
        in_specs=in_specs,
        out_specs=VMEM if single else [VMEM] * len(out_shape),
        scratch_shapes=list(scratch),
        compiler_params=pltpu.CompilerParams(vmem_limit_bytes=mib << 20),
        interpret=INTERPRET,
    )


def shape(*dims):
    return jax.ShapeDtypeStruct(dims, F32)


def tables(length):
    half = length // 2
    k = np.arange(half)[:, None]
    j = np.arange(half)[None, :]
    out = []
    for order in (2 * j, 2 * j + 1):
        angle = (k * order % length).astype(np.float64) * (2.0 * np.pi / length)
        c, s = np.cos(angle) / np.sqrt(length), np.sin(angle) / np.sqrt(length)
        block = np.block([[c, -s], [s, c]]).astype(np.float32)
        for table in (block, block.T):
            high = table.astype(BF16)
            out += [high, (table - high.astype(np.float32)).astype(BF16)]
    return np.stack(out)


def parity_order(length):
    half = length // 2
    order = np.zeros((length, length), np.float32)
    for q in range(2):
        order[2 * np.arange(half) + q, q * half + np.arange(half)] = 1.0
    return np.stack([order, order.T]).astype(BF16)


def halves(value):
    high = value.astype(BF16)
    low = (value - high.astype(F32)).astype(BF16)
    return high, low


def from_left(tab, which, value):
    high, low = halves(value)
    return jnp.dot(
        jnp.concatenate([tab[which], tab[which], tab[which + 1]], axis=1),
        jnp.concatenate([high, low, high], axis=0),
        preferred_element_type=F32,
    )


def from_right(value, tab, which):
    high, low = halves(value)
    return jnp.dot(
        jnp.concatenate([high, low, high], axis=1),
        jnp.concatenate([tab[which], tab[which], tab[which + 1]], axis=0),
        preferred_element_type=F32,
    )


def to_detector(tab, real, imag):
    h = real.shape[0] // 2
    cols = []
    for q in range(2):
        join = jnp.add if q == 0 else jnp.subtract
        pair = [join(v[:, :h], v[:, h:]) for v in (real, imag)]
        cols.append(from_right(jnp.concatenate(pair, axis=1), tab, 4 * q))
    out = []
    for p in range(2):
        join = jnp.add if p == 0 else jnp.subtract
        even, odd = [join(v[:h], v[h:]) for v in cols]
        data = jnp.concatenate(
            [
                jnp.concatenate([even[:, :h], odd[:, :h]], axis=1),
                jnp.concatenate([even[:, h:], odd[:, h:]], axis=1),
            ],
            axis=0,
        )
        out.append(from_left(tab, 4 * p + 2, data))
    return out


def to_sample(tab, even, odd):
    h = even.shape[0] // 2
    a = from_left(tab, 0, even)
    b = from_left(tab, 4, odd)
    top, low = a + b, a - b
    cols = []
    for q in range(2):
        lanes = slice(q * h, (q + 1) * h)
        data = jnp.concatenate(
            [
                jnp.concatenate([top[:h, lanes], low[:h, lanes]], axis=0),
                jnp.concatenate([top[h:, lanes], low[h:, lanes]], axis=0),
            ],
            axis=1,
        )
        cols.append(from_right(data, tab, 4 * q + 2))
    a, b = cols
    real = jnp.concatenate([a[:, :h] + b[:, :h], a[:, :h] - b[:, :h]], axis=1)
    imag = jnp.concatenate([a[:, h:] + b[:, h:], a[:, h:] - b[:, h:]], axis=1)
    return real, imag


def thirds(value):
    high = value.astype(BF16)
    left = value - high.astype(F32)
    mid = left.astype(BF16)
    return high, mid, (left - mid.astype(F32)).astype(BF16)


def amplitude_kernel(amp, order, out):
    slots, size = amp.shape[:2]
    half = size // 2
    for slot in range(slots):
        value = jnp.dot(
            jnp.concatenate(thirds(amp[slot] * 2.0**-8), axis=1),
            jnp.concatenate([order[0]] * 3, axis=0),
            preferred_element_type=F32,
        )
        value = jnp.dot(
            jnp.concatenate([order[1]] * 3, axis=1),
            jnp.concatenate(thirds(value), axis=0),
            preferred_element_type=F32,
        )
        for p in range(2):
            out[slot, p] = value[p * half : (p + 1) * half] * 2.0**8


def cut_kernel(offs, own, following, *pieces):
    half = own.shape[1]
    size = pieces[0].shape[2]
    row = lax.axis_index("obj") * half + lax.broadcasted_iota(jnp.int32, (half, size), 0)
    column = lax.broadcasted_iota(jnp.int32, (half, size), 1)
    for slot, piece in enumerate(pieces):
        here = row >= offs[slot, 0]
        inside = column >= offs[slot, 1]
        for part in range(2):
            near = jnp.where(here, own[part, :, :size], following[part, :, :size])
            far = jnp.where(here, own[part, :, size:], following[part, :, size:])
            piece[part] = jnp.where(inside, near, far)


def shifts(offs, slot, size, half):
    row = lax.rem(offs[slot, 0] - half * lax.axis_index("obj") + size, size)
    return row, lax.rem(offs[slot, 1], size)


def turned(value, rows, columns):
    return pltpu.roll(pltpu.roll(value, rows, 0), columns, 1)


def own_diff():
    return lax.axis_index("chip") * lax.axis_size("core") + lax.axis_index("core")


def slot_kernel(slot, last, offs, counts, mine, theirs, own, other_a, other_b, amp, tab, *rest):
    if last:
        before, grad_keep, grad_send, patch_grad, rest_far, field, far, grads, power = rest
    else:
        grads, patch_grad, rest_far, field, far, _, power = rest
    size = own.shape[-1]
    half = size // 2
    down, across = shifts(offs, slot, size, mine.shape[1])
    weight = (slot < counts[own_diff()]).astype(F32)
    for part in range(2):
        whole = jnp.concatenate([mine[part], theirs[part]], axis=0)
        field[part] = turned(whole, lax.rem(size - down, size), lax.rem(size - across, size))
    modes = (own.at[0], own.at[1], other_a, other_b)

    for mode in range(4):
        pr, pi = modes[mode][0], modes[mode][1]
        fr, fi = field[0], field[1]
        waves = to_detector(tab, pr * fr - pi * fi, pr * fi + pi * fr)
        for p in range(2):
            far[mode, p] = waves[p]
            amount = waves[p][:half] * waves[p][:half] + waves[p][half:] * waves[p][half:]
            power[p] = amount if mode == 0 else power[p] + amount
    for p in range(2):
        power[p] = amp[slot, p] / jnp.sqrt(power[p] + 1.0) - 1.0
    for mode in range(2):
        for p in range(2):
            for part in range(2):
                rows = slice(part * half, (part + 1) * half)
                rest_far[mode, p, rows] = far[2 + mode, p, rows] * power[p]

    for mode in range(2):
        scaled = [
            far[mode, p] * jnp.concatenate([power[p], power[p]], axis=0) for p in range(2)
        ]
        real, imag = to_sample(tab, *scaled)
        pr, pi = modes[mode][0], modes[mode][1]
        fr, fi = field[0], field[1]
        if mode == 0:
            patch_grad[0] = pr * real + pi * imag
            patch_grad[1] = pr * imag - pi * real
        else:
            patch_grad[0] += pr * real + pi * imag
            patch_grad[1] += pr * imag - pi * real
        grads[mode, 0] = weight * (fr * real + fi * imag)
        grads[mode, 1] = weight * (fr * imag - fi * real)
    if last:
        core = lax.axis_index("core")
        grad_keep[...] = before[core] + grads[core]
        grad_send[...] = before[1 - core] + grads[1 - core]


def spread_kernel(offs, counts, other_a, other_b, tab, grad_0, far_0, grad_1, far_1, own, spill, total):
    half = own.shape[1]
    size = total.shape[-1]
    row = lax.axis_index("obj") * half + lax.broadcasted_iota(jnp.int32, (half, size), 0)
    column = lax.broadcasted_iota(jnp.int32, (half, size), 1)
    for slot, (grad, far) in enumerate(((grad_0, far_0), (grad_1, far_1))):
        total[...] = grad[...]
        for mode, other in enumerate((other_a, other_b)):
            real, imag = to_sample(tab, far[mode, 0], far[mode, 1])
            pr, pi = other[0], other[1]
            total[0] += pr * real + pi * imag
            total[1] += pr * imag - pi * real
        down, across = shifts(offs, slot, size, half)
        here = row >= offs[slot, 0]
        inside = column >= offs[slot, 1]
        weight = (slot < counts[own_diff()]).astype(F32)
        for part in range(2):
            value = weight * turned(total[part], down, across)[:half]
            stay = jnp.where(here, value, 0.0)
            leave = value - stay
            for target, amount in ((own, stay), (spill, leave)):
                near = jnp.where(inside, amount, 0.0)
                if slot == 0:
                    target[part, :, :size] = near
                    target[part, :, size:] = amount - near
                else:
                    target[part, :, :size] += near
                    target[part, :, size:] += amount - near


def diffuse_kernel(total_rows, above, tile, below, out):
    rows = tile.shape[1]
    columns = tile.shape[2]
    flat = own_diff() * lax.axis_size("obj") + lax.axis_index("obj")
    full = rows + 2 * HALO
    row = flat * rows - HALO + lax.broadcasted_iota(jnp.int32, (full, columns), 0)
    column = lax.broadcasted_iota(jnp.int32, (full, columns), 1)
    has_below = (row >= 0) & (row < total_rows - 1)
    has_right = column < columns - 1
    now = [jnp.concatenate([above[p], tile[p], below[p]], axis=0) for p in range(2)]

    def flux(axis, length, valid):
        step = [pltpu.roll(v, length - 1, axis) - v for v in now]
        weight = 1.0 / (1.0 + (step[0] * step[0] + step[1] * step[1]) / (EDGE_SCALE * EDGE_SCALE))
        weight = jnp.where(valid, weight, 0.0)
        step = [s * weight for s in step]
        return [s - pltpu.roll(s, 1, axis) for s in step]

    for _ in range(PASSES):
        vertical = flux(0, full, has_below)
        sideways = flux(1, columns, has_right)
        now = [u + DIFFUSION_RATE * (v + s) for u, v, s in zip(now, vertical, sideways)]
    for p in range(2):
        out[p] = now[p][HALO : HALO + rows]


def shifted(value, axes, count, steps):
    return lax.ppermute(
        value, axes, [(i, i + steps) for i in range(count) if 0 <= i + steps < count]
    )


def body(object_field, probe_modes, amplitudes, offsets, counts):
    tile_rows, columns = object_field.shape[1:]
    size = probe_modes.shape[-1]
    n_chip, n_core, n_obj = (lax.axis_size(a) for a in ("chip", "core", "obj"))
    n_diff = n_chip * n_core
    total_rows = tile_rows * n_obj * n_diff
    core = lax.axis_index("core")
    swap = [(0, 1), (1, 0)]
    tab = jnp.asarray(tables(size))

    following = shifted(object_field, DIFF, n_diff, -1)
    mode = lax.dynamic_index_in_dim(probe_modes, core, 0, keepdims=False)
    other_a = lax.ppermute(mode, DIFF + ("obj",), probe_pairs(n_chip, n_obj))
    other_b = lax.ppermute(other_a, "core", swap)
    amp = call(
        amplitude_kernel, shape(amplitudes.shape[0], 2, size // 2, size), [VMEM, VMEM]
    )(amplitudes, jnp.asarray(parity_order(size)))
    piece = shape(2, tile_rows, size)
    mine = call(cut_kernel, [piece, piece], [SMEM, VMEM, VMEM])(offsets, object_field, following)
    theirs_0 = lax.ppermute(mine[0], "obj", swap)
    theirs_1 = lax.ppermute(mine[1], "obj", swap)

    both = shape(2, 2, size, size)
    patch = shape(2, size, size)
    scratch = [
        pltpu.VMEM((2, size, size), F32),
        pltpu.VMEM((4, 2, size, size), F32),
        pltpu.VMEM((2, 2, size, size), F32),
        pltpu.VMEM((2, size // 2, size), F32),
    ]
    specs = [SMEM, SMEM] + [VMEM] * 7
    grads, patch_0, far_0 = call(
        functools.partial(slot_kernel, 0, False),
        [both, patch, both], specs, scratch, 24,
    )(offsets, counts, mine[0], theirs_0, probe_modes, other_a, other_b, amp, tab)
    keep, send, patch_1, far_1 = call(
        functools.partial(slot_kernel, 1, True),
        [patch, patch, patch, both], specs + [VMEM], scratch, 24,
    )(offsets, counts, mine[1], theirs_1, probe_modes, other_a, other_b, amp, tab, grads)

    summed = keep + lax.ppermute(send, "core", swap)
    pieces = summed.reshape(n_chip, 2 * size // n_chip, size)
    gathered = lax.all_to_all(pieces, "chip", 0, 0)
    share = jnp.sum(gathered, axis=0)
    views = probe_modes.reshape(2, n_chip, 2 * size // n_chip, size)
    start = lax.dynamic_slice(
        views, (core, lax.axis_index("chip"), 0, 0), (1, 1) + views.shape[2:]
    )[0, 0]
    share = start + share / n_diff
    updated = lax.all_to_all(jnp.broadcast_to(share[None], pieces.shape), "chip", 0, 0)
    updated = updated.reshape(2, size, size)
    remote = lax.ppermute(updated, "core", swap)
    probe_out = jnp.where(
        core == 0, jnp.stack([updated, remote]), jnp.stack([remote, updated])
    )

    tile = shape(2, tile_rows, columns)
    own, spill = call(
        spread_kernel,
        [tile, tile],
        [SMEM, SMEM] + [VMEM] * 7,
        [pltpu.VMEM((2, size, size), F32)],
        16,
    )(offsets, counts, other_a, other_b, tab, patch_0, far_0, patch_1, far_1)
    arrived = shifted(spill, DIFF, n_diff, 1)
    raised = object_field + OBJECT_STEP * (own + arrived)
    flat = DIFF + ("obj",)
    above = shifted(raised[:, tile_rows - HALO :], flat, n_diff * n_obj, 1)
    below = shifted(raised[:, :HALO], flat, n_diff * n_obj, -1)
    smooth = call(
        functools.partial(diffuse_kernel, total_rows), tile, [VMEM] * 3, ()
    )(above, raised, below)
    return smooth, probe_out


def probe_pairs(n_chip, n_obj):
    def place(chip, core, obj):
        return (chip * 2 + core) * n_obj + obj

    return [
        (place(chip, core, obj), place(chip ^ core, core, 1 - obj))
        for chip in range(n_chip)
        for core in range(2)
        for obj in range(n_obj)
    ]


def solution(mesh):
    n_diff, n_obj = mesh.devices.shape
    fine = Mesh(mesh.devices.reshape(n_diff // 2, 2, n_obj), ("chip", "core", "obj"))
    placed = (
        P(None, ("chip", "core", "obj"), None),
        P("obj", None, None, None),
        P(DIFF, None, None),
        P(DIFF, None),
        P(),
    )
    return jax.shard_map(
        body,
        mesh=fine,
        in_specs=placed,
        out_specs=(P(None, ("chip", "core", "obj"), None), P("obj", None, None, None)),
        check_vma=False,
    )
```

time: 1620 us -> 125 us (0.08); the launches traced: 1600 us -> 124 us
  waiting for transfers between devices: 1440 us -> 53.1 us
  matrix products: 61 us -> 0 us
  Pallas kernels: 0 us -> 18.3 us
    psum x3 -> x0, waiting for transfers between devices: 1330 us -> none  [the longest x1 1260 us: body(): probe_total = lax.psum(probe_grad_sum, 'diff')]
    dot_general x32 -> x0, matrix products: 61 us -> none  [the longest x16 31.2 us: apply_right(): return jnp.einsum('mjk,kl->mjl', stacked, table, precision=HIGHEST)]
    all_gather x1 -> x0, waiting for transfers between devices: 29.8 us -> none  [body(): block = lax.all_gather(object_field, 'obj', axis=1, tiled=True)]
    reduce_scatter x1 -> x0, waiting for transfers between devices: 22.7 us -> none  [body(): lax.psum_scatter(grad_ext[:, :block_rows] + spilled, 'obj', scatter_dimen...]
    all_to_all x0 -> x2, waiting for transfers between devices: none -> 21.3 us  [the longest x1 16.3 us: body(): gathered = lax.all_to_all(pieces, 'chip', 0, 0)]
    all_to_all x0 -> x2, starting transfers between devices: none -> 20.5 us  [the longest x1 11.3 us: body(): gathered = lax.all_to_all(pieces, 'chip', 0, 0)]
    ppermute x8 -> x10, waiting for transfers between devices: 50.3 us -> 31.8 us  [the longest x4 16.2 us: shifted(): lax.ppermute(value, axes, [(i, i + steps) for i in range(count) if 0 <= i...]
    pallas_call x0 -> x6, Pallas kernels: none -> 18.3 us  [the longest x1 5.24 us: body(): call(functools.partial(slot_kernel, 1, True), [patch, patch, patch, both]...]
  transfers between devices with their start and end apart: 13 -> 12, of which waited for: 10 -> 8; matrix products, arithmetic and copies ran while one was open for 1% -> 1% of each run, Pallas kernels for 0% -> 11%
where the time goes in v1:
time: 125 us; the launch traced here: 124 us
  waiting for transfers between devices  53.1 us (42%)
  starting transfers between devices  38.9 us (31%)
  Pallas kernels  18.3 us (15%)
  local copies, waits for them, and re-layouts  7.33 us (6%)
  other arithmetic  5.46 us (4%)
    all_to_all x1, waiting for transfers between devices, body(): gathered = lax.all_to_all(pieces, 'chip', 0, 0)  16.3 us
    ppermute x4, waiting for transfers between devices, shifted(): lax.ppermute(value, axes, [(i, i + steps) for i in range(count) if 0 <= i...  16.2 us
    ppermute x4, starting transfers between devices, shifted(): lax.ppermute(value, axes, [(i, i + steps) for i in range(count) if 0 <= i...  12.7 us
    all_to_all x1, starting transfers between devices, body(): gathered = lax.all_to_all(pieces, 'chip', 0, 0)  11.3 us
    all_to_all x1, starting transfers between devices, body(): lax.all_to_all(jnp.broadcast_to(share[None], pieces.shape), 'chip', 0, 0)  9.2 us
    ppermute x1, waiting for transfers between devices, body(): other_a = lax.ppermute(mode, DIFF + ('obj',), probe_pairs(n_chip, n_obj))  8.22 us
    ppermute x1, waiting for transfers between devices, body(): theirs_0 = lax.ppermute(mine[0], 'obj', swap)  5.35 us
    unnamed x34, local copies, waits for them, and re-layouts  5.31 us
  transfers between devices with their start and end apart: 12, of which 8 were waited for; matrix products, arithmetic and copies ran while one was open for 1% of the time, Pallas kernels for 11%

profile of v1, /device:TPU:128, one launch (start us, length us, event | category | flops | bytes accessed | tf_op | source)
XLA Modules:
  0.0 124.0 jit_solution(15125677099509910421)
XLA Ops:
  0.6 0.0 copy-start.2
  0.7 0.0 copy-start.14
  0.7 1.2 dynamic-slice_bitcast_fusion
  1.9 0.0 copy-start
  1.9 0.0 copy-start.1
  1.9 1.7 %collective-permute-start = (f32[2,256,256]{2,1,0:T(8,128)S(1)}, f32[2,256,256]{2,1,0:T(8,128)S(1)}, u32[]{:S(2)}, u32[]{:S(2)}) collective-permute-start(f32[2,256,256]{2,1,0:T(8,128)S(1)} %dynamic-slice_bitcast_fusion), channel_id=1, source_target_pairs={{0,1},{1,0},{2,7},{3,6},{4,5},{5,4},{6,3},{7,2},{8,9},{9,8},{10,15... | collective-permute-start | bytes 1572872 | tf_op jit(solution)/shard_map/ppermute | solution.py:311
  3.6 5.0 %collective-permute-start.2 = (f32[2,128,512]{2,1,0:T(8,128)S(1)}, f32[2,128,512]{2,1,0:T(8,128)S(1)}, u32[]{:S(2)}, u32[]{:S(2)}) collective-permute-start(f32[2,128,512]{2,1,0:T(8,128)S(1)} %copy-done.2), channel_id=1, source_target_pairs={{2,0},{4,2},{6,4},{8,6},{10,8},{12,10},{14,12},{16,14},{18,16},{20... | collective-permute-start | bytes 1572872 | tf_op jit(solution)/shard_map/ppermute | solution.py:294
  8.6 8.2 %collective-permute-done.other_a = f32[2,256,256]{2,1,0:T(8,128)S(1)} collective-permute-done((f32[2,256,256]{2,1,0:T(8,128)S(1)}, f32[2,256,256]{2,1,0:T(8,128)S(1)}, u32[]{:S(2)}, u32[]{:S(2)}) %collective-permute-start) | collective-permute-done | bytes 524320 | tf_op jit(solution)/shard_map/ppermute | solution.py:311
  16.8 0.0 collective-permute-start.1
  16.8 0.0 collective-permute-done.2.following
  16.8 0.7 shard_map.86
  17.5 1.7 %collective-permute-start.3 = (f32[2,128,256]{2,1,0:T(8,128)S(1)}, f32[2,128,256]{2,1,0:T(8,128)S(1)}, u32[]{:S(2)}, u32[]{:S(2)}) collective-permute-start(f32[2,128,256]{2,1,0:T(8,128)S(1)} %get-tuple-element.13.mine), channel_id=1, source_target_pairs={{0,1},{1,0},{2,3},{3,2},{4,5},{5,4},{6,7},{7,6},{8,9},{9,8},{10,11... | collective-permute-start | bytes 786440 | tf_op jit(solution)/shard_map/ppermute | solution.py:318
  19.2 0.4 collective-permute-start.4
  19.6 0.9 shard_map.87.amp
  20.5 5.4 %collective-permute-done.3.theirs = f32[2,128,256]{2,1,0:T(8,128)S(1)} collective-permute-done((f32[2,128,256]{2,1,0:T(8,128)S(1)}, f32[2,128,256]{2,1,0:T(8,128)S(1)}, u32[]{:S(2)}, u32[]{:S(2)}) %collective-permute-start.3) | collective-permute-done | bytes 262176 | tf_op jit(solution)/shard_map/ppermute | solution.py:318
  25.8 0.0 collective-permute-done.1.other_b
  25.9 5.1 %shard_map.88 = (f32[2,2,256,256]{3,2,1,0:T(8,128)S(1)}, f32[2,256,256]{2,1,0:T(8,128)S(1)}, f32[2,2,256,256]{3,2,1,0:T(8,128)S(1)}) custom-call(s32[2,2]{1,0:T(2,128)S(1)} %copy-done.15, s32[128]{0:T(128)S(1)} %copy-done.16, f32[2,128,256]{2,1,0:T(8,128)S(1)} %get-tuple-element.13.mine, f32[2,128,256]{2,1,0:T(8,128)S(1)} %collective-permute-done.3.theirs, ...), custom_call_target="tpu_custom_call" | custom-call | tf_op jit(solution)/shard_map/pallas_call | solution.py:330
  31.0 0.0 copy-start.4
  31.0 0.0 copy-start.8
  31.0 0.4 collective-permute-done.4.theirs
  31.5 5.2 %shard_map.89 = (f32[2,256,256]{2,1,0:T(8,128)S(1)}, f32[2,256,256]{2,1,0:T(8,128)S(1)}, f32[2,256,256]{2,1,0:T(8,128)S(1)}, f32[2,2,256,256]{3,2,1,0:T(8,128)S(1)}) custom-call(s32[2,2]{1,0:T(2,128)S(1)} %copy-done.15, s32[128]{0:T(128)S(1)} %copy-done.16, f32[2,128,256]{2,1,0:T(8,128)S(1)} %get-tuple-element.16.mine, ...), custom_call_target="tpu_custom_call" | custom-call | tf_op jit(solution)/shard_map/pallas_call | solution.py:334
  36.7 1.0 copy-done.6
  37.7 1.9 %collective-permute-start.8 = (f32[2,256,256]{2,1,0:T(8,128)S(1)}, f32[2,256,256]{2,1,0:T(8,128)S(1)}, u32[]{:S(2)}, u32[]{:S(2)}) collective-permute-start(f32[2,256,256]{2,1,0:T(8,128)S(1)} %get-tuple-element.23), channel_id=1, source_target_pairs={{0,2},{2,0},{1,3},{3,1},{4,6},{6,4},{5,7},{7,5},{8,10},{10,8},{9,1... | collective-permute-start | bytes 1572872 | tf_op jit(solution)/shard_map/ppermute | solution.py:339
  39.6 1.5 %collective-permute-done.8 = f32[2,256,256]{2,1,0:T(8,128)S(1)} collective-permute-done((f32[2,256,256]{2,1,0:T(8,128)S(1)}, f32[2,256,256]{2,1,0:T(8,128)S(1)}, u32[]{:S(2)}, u32[]{:S(2)}) %collective-permute-start.8) | collective-permute-done | bytes 524320 | tf_op jit(solution)/shard_map/ppermute | solution.py:339
  41.1 0.9 add.28
  42.0 11.3 %all-to-all-start = ((f32[64,8,256]{2,1,0:T(8,128)}), f32[64,8,256]{2,1,0:T(8,128)}, u32[]{:S(2)}, u32[]{:S(2)}) async-start(f32[64,8,256]{2,1,0:T(8,128)} %bitcast.10), calls=%async_computation | async-start | bytes 1048576 | tf_op jit(solution)/shard_map/all_to_all | solution.py:341
  53.3 16.3 %all-to-all-done = f32[64,8,256]{2,1,0:T(8,128)} async-done(((f32[64,8,256]{2,1,0:T(8,128)}), f32[64,8,256]{2,1,0:T(8,128)}, u32[]{:S(2)}, u32[]{:S(2)}) %all-to-all-start) | async-done | bytes 524320 | tf_op jit(solution)/shard_map/all_to_all | solution.py:341
  69.6 1.1 reduce_sum.9
  70.7 0.8 broadcast_in_dim.2
  71.6 9.2 %all-to-all-start.1 = ((f32[64,8,256]{2,1,0:T(8,128)}), f32[64,8,256]{2,1,0:T(8,128)}, u32[]{:S(2)}, u32[]{:S(2)}) async-start(f32[64,8,256]{2,1,0:T(8,128)} %broadcast_in_dim.2), calls=%async_computation.1 | async-start | bytes 1048576 | tf_op jit(solution)/shard_map/all_to_all | solution.py:348
  80.8 0.0 copy-start.5
  80.8 1.2 copy-done.5
  82.0 1.2 copy-done.7
  83.3 1.0 copy-done.11
  84.3 4.2 %shard_map.90 = (f32[2,128,512]{2,1,0:T(8,128)S(1)}, f32[2,128,512]{2,1,0:T(8,128)}) custom-call(s32[2,2]{1,0:T(2,128)S(1)} %copy-done.15, s32[128]{0:T(128)S(1)} %copy-done.16, f32[2,256,256]{2,1,0:T(8,128)S(1)} %collective-permute-done.other_a, f32[2,256,256]{2,1,0:T(8,128)S(1)} %collective-permute-done.1.other_b, bf16[8,256,256]{2,1,0:T(8,128)(2,1)S(1)} %copy-done, ...), custom_call_target="tpu_custom_call" | custom-call | tf_op jit(solution)/shard_map/pallas_call | solution.py:356
  88.5 0.8 copy-done.13
  89.3 1.9 %collective-permute-start.5 = (f32[2,128,512]{2,1,0:T(8,128)}, f32[2,128,512]{2,1,0:T(8,128)S(1)}, u32[]{:S(2)}, u32[]{:S(2)}) collective-permute-start(f32[2,128,512]{2,1,0:T(8,128)} %get-tuple-element.21), channel_id=1, source_target_pairs={{0,2},{2,4},{4,6},{6,8},{8,10},{10,12},{12,14},{14,16},{16,18},{18... | collective-permute-start | bytes 1572872 | tf_op jit(solution)/shard_map/ppermute | solution.py:294
  91.2 5.0 %all-to-all-done.1 = f32[64,8,256]{2,1,0:T(8,128)} async-done(((f32[64,8,256]{2,1,0:T(8,128)}), f32[64,8,256]{2,1,0:T(8,128)}, u32[]{:S(2)}, u32[]{:S(2)}) %all-to-all-start.1) | async-done | bytes 524320 | tf_op jit(solution)/shard_map/all_to_all | solution.py:348
  96.2 0.0 collective-permute-start.9
  96.2 9.5 %collective-permute-done.5 = f32[2,128,512]{2,1,0:T(8,128)S(1)} collective-permute-done((f32[2,128,512]{2,1,0:T(8,128)}, f32[2,128,512]{2,1,0:T(8,128)S(1)}, u32[]{:S(2)}, u32[]{:S(2)}) %collective-permute-start.5) | collective-permute-done | bytes 524320 | tf_op jit(solution)/shard_map/ppermute | solution.py:294
  105.7 1.2 multiply_add_fusion.tile
  106.9 1.9 %collective-permute-start.7 = (f32[2,8,512]{2,1,0:T(8,128)S(1)}, f32[2,8,512]{2,1,0:T(8,128)S(1)}, u32[]{:S(2)}, u32[]{:S(2)}) collective-permute-start(f32[2,8,512]{2,1,0:T(8,128)S(1)} %get-tuple-element.24), channel_id=1, source_target_pairs={{1,0},{2,1},{3,2},{4,3},{5,4},{6,5},{7,6},{8,7},{9,8},{10,9},{11,1... | collective-permute-start | bytes 98312 | tf_op jit(solution)/shard_map/ppermute | solution.py:294
  108.8 3.9 %collective-permute-start.6 = (f32[2,8,512]{2,1,0:T(8,128)S(1)}, f32[2,8,512]{2,1,0:T(8,128)S(1)}, u32[]{:S(2)}, u32[]{:S(2)}) collective-permute-start(f32[2,8,512]{2,1,0:T(8,128)S(1)} %get-tuple-element.25), channel_id=1, source_target_pairs={{0,1},{1,2},{2,3},{3,4},{4,5},{5,6},{6,7},{7,8},{8,9},{9,10},{10,1... | collective-permute-start | bytes 98312 | tf_op jit(solution)/shard_map/ppermute | solution.py:294
  112.8 0.0 collective-permute-done.7.below
  112.8 6.7 %collective-permute-done.6.above = f32[2,8,512]{2,1,0:T(8,128)S(1)} collective-permute-done((f32[2,8,512]{2,1,0:T(8,128)S(1)}, f32[2,8,512]{2,1,0:T(8,128)S(1)}, u32[]{:S(2)}, u32[]{:S(2)}) %collective-permute-start.6) | collective-permute-done | bytes 32800 | tf_op jit(solution)/shard_map/ppermute | solution.py:294
  119.5 2.2 %shard_map.91 = f32[2,128,512]{2,1,0:T(8,128)} custom-call(f32[2,8,512]{2,1,0:T(8,128)S(1)} %collective-permute-done.6.above, f32[2,128,512]{2,1,0:T(8,128)S(1)} %multiply_add_fusion.tile, f32[2,8,512]{2,1,0:T(8,128)S(1)} %collective-permute-done.7.below), custom_call_target="tpu_custom_call" | custom-call | tf_op jit(solution)/shard_map/pallas_call | solution.py:368
  121.7 0.0 collective-permute-done.9
  121.7 2.3 %maximum_select_fusion = f32[2,2,256,256]{3,2,1,0:T(8,128)} fusion(f32[1,2,256,256]{3,2,1,0:T(8,128)S(1)} %bitcast.11, f32[1,2,256,256]{3,2,1,0:T(8,128)} %bitcast.4, pred[]{:T(512)S(6)} %eq.3), kind=kLoop, calls=%fused_computation | loop fusion | flops 786432 | bytes 2097153 | tf_op jit(solution)/shard_map/jit(_where)/select_n | solution.py:351
  (24 shorter events, 0.1 us)
Async XLA Ops:
  0.6 16.1 %copy-start.15 = (s32[2,2]{1,0:T(2,128)S(1)}, s32[2,2]{1,0:T(2,128)}, u32[]{:S(2)}) copy-start(s32[2,2]{1,0:T(2,128)} %offs.7) | copy-start | bytes 52
  0.6 2.9 %copy-start.2 = (f32[2,128,512]{2,1,0:T(8,128)S(1)}, f32[2,128,512]{2,1,0:T(8,128)}, u32[]{:S(2)}) copy-start(f32[2,128,512]{2,1,0:T(8,128)} %own.3) | copy-start | bytes 1572868
  0.7 18.9 %copy-start.12 = (f32[2,256,256]{2,1,0:T(8,128)S(1)}, f32[2,256,256]{2,1,0:T(8,128)}, u32[]{:S(2)}) copy-start(f32[2,256,256]{2,1,0:T(8,128)} %amp.1) | copy-start | bytes 1572868
  0.7 18.9 %copy-start.14 = (bf16[2,256,256]{2,1,0:T(8,128)(2,1)S(1)}, bf16[2,256,256]{2,1,0:T(8,128)(2,1)}, u32[]{:S(2)}) copy-start(bf16[2,256,256]{2,1,0:T(8,128)(2,1)} %constant.32.clone.order) | copy-start | bytes 786436
  1.9 24.0 %copy-start = (bf16[8,256,256]{2,1,0:T(8,128)(2,1)S(1)}, bf16[8,256,256]{2,1,0:T(8,128)(2,1)}, u32[]{:S(2)}) copy-start(bf16[8,256,256]{2,1,0:T(8,128)(2,1)} %constant.31.clone.tab) | copy-start | bytes 3145732
  1.9 24.0 %copy-start.1 = (f32[2,2,256,256]{3,2,1,0:T(8,128)S(1)}, f32[2,2,256,256]{3,2,1,0:T(8,128)}, u32[]{:S(2)}) copy-start(f32[2,2,256,256]{3,2,1,0:T(8,128)} %own.5) | copy-start | bytes 3145732
  1.9 14.9 %collective-permute-start = (f32[2,256,256]{2,1,0:T(8,128)S(1)}, f32[2,256,256]{2,1,0:T(8,128)S(1)}, u32[]{:S(2)}, u32[]{:S(2)}) collective-permute-start(f32[2,256,256]{2,1,0:T(8,128)S(1)} %dynamic-slice_bitcast_fusion), channel_id=1, source_target_pairs={{0,1},{1,0},{2,7},{3,6},{4,5},{5,4},{6,3},{7,2},{8,9},{9,8},{10,15... | collective-permute-start | bytes 1572872 | tf_op jit(solution)/shard_map/ppermute | solution.py:311
  3.6 13.2 %collective-permute-start.2 = (f32[2,128,512]{2,1,0:T(8,128)S(1)}, f32[2,128,512]{2,1,0:T(8,128)S(1)}, u32[]{:S(2)}, u32[]{:S(2)}) collective-permute-start(f32[2,128,512]{2,1,0:T(8,128)S(1)} %copy-done.2), channel_id=1, source_target_pairs={{2,0},{4,2},{6,4},{8,6},{10,8},{12,10},{14,12},{16,14},{18,16},{20... | collective-permute-start | bytes 1572872 | tf_op jit(solution)/shard_map/ppermute | solution.py:294
  16.8 9.1 %collective-permute-start.1 = (f32[2,256,256]{2,1,0:T(8,128)S(1)}, f32[2,256,256]{2,1,0:T(8,128)S(1)}, u32[]{:S(2)}, u32[]{:S(2)}) collective-permute-start(f32[2,256,256]{2,1,0:T(8,128)S(1)} %collective-permute-done.other_a), channel_id=1, source_target_pairs={{0,2},{2,0},{1,3},{3,1},{4,6},{6,4},{5,7},{7,5},{8,10},{10,8},{9,1... | collective-permute-start | bytes 1572872 | tf_op jit(solution)/shard_map/ppermute | solution.py:312
  17.5 8.4 %collective-permute-start.3 = (f32[2,128,256]{2,1,0:T(8,128)S(1)}, f32[2,128,256]{2,1,0:T(8,128)S(1)}, u32[]{:S(2)}, u32[]{:S(2)}) collective-permute-start(f32[2,128,256]{2,1,0:T(8,128)S(1)} %get-tuple-element.13.mine), channel_id=1, source_target_pairs={{0,1},{1,0},{2,3},{3,2},{4,5},{5,4},{6,7},{7,6},{8,9},{9,8},{10,11... | collective-permute-start | bytes 786440 | tf_op jit(solution)/shard_map/ppermute | solution.py:318
  19.2 6.7 %copy-start.16 = (s32[128]{0:T(128)S(1)}, s32[128]{0:T(128)}, u32[]{:S(2)}) copy-start(s32[128]{0:T(128)} %counts.5) | copy-start | bytes 1540
  19.2 12.3 %collective-permute-start.4 = (f32[2,128,256]{2,1,0:T(8,128)S(1)}, f32[2,128,256]{2,1,0:T(8,128)S(1)}, u32[]{:S(2)}, u32[]{:S(2)}) collective-permute-start(f32[2,128,256]{2,1,0:T(8,128)S(1)} %get-tuple-element.16.mine), channel_id=1, source_target_pairs={{0,1},{1,0},{2,3},{3,2},{4,5},{5,4},{6,7},{7,6},{8,9},{9,8},{10,11... | collective-permute-start | bytes 786440 | tf_op jit(solution)/shard_map/ppermute | solution.py:319
  31.0 5.7 %copy-start.4 = (f32[2,2,256,256]{3,2,1,0:T(8,128)}, f32[2,2,256,256]{3,2,1,0:T(8,128)S(1)}, u32[]{:S(2)}) copy-start(f32[2,2,256,256]{3,2,1,0:T(8,128)S(1)} %get-tuple-element.15.far_0) | copy-start | bytes 3145732
  31.0 5.7 %copy-start.8 = (f32[2,256,256]{2,1,0:T(8,128)}, f32[2,256,256]{2,1,0:T(8,128)S(1)}, u32[]{:S(2)}) copy-start(f32[2,256,256]{2,1,0:T(8,128)S(1)} %get-tuple-element.14.grad_0) | copy-start | bytes 1572868
  36.7 1.0 copy-start.6
  37.7 4.3 %copy-start.10 = (f32[2,256,256]{2,1,0:T(8,128)}, f32[2,256,256]{2,1,0:T(8,128)S(1)}, u32[]{:S(2)}) copy-start(f32[2,256,256]{2,1,0:T(8,128)S(1)} %get-tuple-element.18.grad_1) | copy-start | bytes 1572868
  37.7 3.4 %collective-permute-start.8 = (f32[2,256,256]{2,1,0:T(8,128)S(1)}, f32[2,256,256]{2,1,0:T(8,128)S(1)}, u32[]{:S(2)}, u32[]{:S(2)}) collective-permute-start(f32[2,256,256]{2,1,0:T(8,128)S(1)} %get-tuple-element.23), channel_id=1, source_target_pairs={{0,2},{2,0},{1,3},{3,1},{4,6},{6,4},{5,7},{7,5},{8,10},{10,8},{9,1... | collective-permute-start | bytes 1572872 | tf_op jit(solution)/shard_map/ppermute | solution.py:339
  42.0 27.6 %all-to-all-start = ((f32[64,8,256]{2,1,0:T(8,128)}), f32[64,8,256]{2,1,0:T(8,128)}, u32[]{:S(2)}, u32[]{:S(2)}) async-start(f32[64,8,256]{2,1,0:T(8,128)} %bitcast.10), calls=%async_computation | async-start | bytes 1048576 | tf_op jit(solution)/shard_map/all_to_all | solution.py:341
  71.6 9.2 %copy-start.9 = (f32[2,256,256]{2,1,0:T(8,128)S(1)}, f32[2,256,256]{2,1,0:T(8,128)}, u32[]{:S(2)}) copy-start(f32[2,256,256]{2,1,0:T(8,128)} %copy-done.8) | copy-start | bytes 1572868
  71.6 24.6 %all-to-all-start.1 = ((f32[64,8,256]{2,1,0:T(8,128)}), f32[64,8,256]{2,1,0:T(8,128)}, u32[]{:S(2)}, u32[]{:S(2)}) async-start(f32[64,8,256]{2,1,0:T(8,128)} %broadcast_in_dim.2), calls=%async_computation.1 | async-start | bytes 1048576 | tf_op jit(solution)/shard_map/all_to_all | solution.py:348
  80.8 1.2 copy-start.5
  82.0 1.2 copy-start.7
  83.3 1.0 copy-start.11
  84.3 21.4 %copy-start.3 = (f32[2,128,512]{2,1,0:T(8,128)S(1)}, f32[2,128,512]{2,1,0:T(8,128)}, u32[]{:S(2)}) copy-start(f32[2,128,512]{2,1,0:T(8,128)} %own.3) | copy-start | bytes 1572868
  88.5 0.8 copy-start.13
  89.3 16.4 %collective-permute-start.5 = (f32[2,128,512]{2,1,0:T(8,128)}, f32[2,128,512]{2,1,0:T(8,128)S(1)}, u32[]{:S(2)}, u32[]{:S(2)}) collective-permute-start(f32[2,128,512]{2,1,0:T(8,128)} %get-tuple-element.21), channel_id=1, source_target_pairs={{0,2},{2,4},{4,6},{6,8},{8,10},{10,12},{12,14},{14,16},{16,18},{18... | collective-permute-start | bytes 1572872 | tf_op jit(solution)/shard_map/ppermute | solution.py:294
  96.2 25.5 %collective-permute-start.9 = (f32[2,256,256]{2,1,0:T(8,128)}, f32[2,256,256]{2,1,0:T(8,128)S(1)}, u32[]{:S(2)}, u32[]{:S(2)}) collective-permute-start(f32[2,256,256]{2,1,0:T(8,128)} %bitcast.5), channel_id=1, source_target_pairs={{0,2},{2,0},{1,3},{3,1},{4,6},{6,4},{5,7},{7,5},{8,10},{10,8},{9,1... | collective-permute-start | bytes 1572872 | tf_op jit(solution)/shard_map/ppermute | solution.py:350
  106.9 5.9 %collective-permute-start.7 = (f32[2,8,512]{2,1,0:T(8,128)S(1)}, f32[2,8,512]{2,1,0:T(8,128)S(1)}, u32[]{:S(2)}, u32[]{:S(2)}) collective-permute-start(f32[2,8,512]{2,1,0:T(8,128)S(1)} %get-tuple-element.24), channel_id=1, source_target_pairs={{1,0},{2,1},{3,2},{4,3},{5,4},{6,5},{7,6},{8,7},{9,8},{10,9},{11,1... | collective-permute-start | bytes 98312 | tf_op jit(solution)/shard_map/ppermute | solution.py:294
  108.8 10.7 %collective-permute-start.6 = (f32[2,8,512]{2,1,0:T(8,128)S(1)}, f32[2,8,512]{2,1,0:T(8,128)S(1)}, u32[]{:S(2)}, u32[]{:S(2)}) collective-permute-start(f32[2,8,512]{2,1,0:T(8,128)S(1)} %get-tuple-element.25), channel_id=1, source_target_pairs={{0,1},{1,2},{2,3},{3,4},{4,5},{5,6},{6,7},{7,8},{8,9},{9,10},{10,1... | collective-permute-start | bytes 98312 | tf_op jit(solution)/shard_map/ppermute | solution.py:294

commit v2 on v1

--- a/solution.py
+++ b/solution.py
@@ -185,9 +185,9 @@
 
 def slot_kernel(slot, last, offs, counts, mine, theirs, own, other_a, other_b, amp, tab, *rest):
     if last:
-        before, grad_keep, grad_send, patch_grad, rest_far, field, far, grads, power = rest
+        before, grad_keep, grad_send, extra, field, far, grads, power = rest
     else:
-        grads, patch_grad, rest_far, field, far, _, power = rest
+        grads, extra, field, far, _, power = rest
     size = own.shape[-1]
     half = size // 2
     down, across = shifts(offs, slot, size, mine.shape[1])
@@ -211,7 +211,7 @@
         for p in range(2):
             for part in range(2):
                 rows = slice(part * half, (part + 1) * half)
-                rest_far[mode, p, rows] = far[2 + mode, p, rows] * power[p]
+                extra[mode, p, rows] = far[2 + mode, p, rows] * power[p]
 
     for mode in range(2):
         scaled = [
@@ -221,11 +221,11 @@
         pr, pi = modes[mode][0], modes[mode][1]
         fr, fi = field[0], field[1]
         if mode == 0:
-            patch_grad[0] = pr * real + pi * imag
-            patch_grad[1] = pr * imag - pi * real
+            extra[2, 0] = pr * real + pi * imag
+            extra[2, 1] = pr * imag - pi * real
         else:
-            patch_grad[0] += pr * real + pi * imag
-            patch_grad[1] += pr * imag - pi * real
+            extra[2, 0] += pr * real + pi * imag
+            extra[2, 1] += pr * imag - pi * real
         grads[mode, 0] = weight * (fr * real + fi * imag)
         grads[mode, 1] = weight * (fr * imag - fi * real)
     if last:
@@ -234,15 +234,15 @@
         grad_send[...] = before[1 - core] + grads[1 - core]
 
 
-def spread_kernel(offs, counts, other_a, other_b, tab, grad_0, far_0, grad_1, far_1, own, spill, total):
+def spread_kernel(offs, counts, other_a, other_b, tab, extra_0, extra_1, own, spill, total):
     half = own.shape[1]
     size = total.shape[-1]
     row = lax.axis_index("obj") * half + lax.broadcasted_iota(jnp.int32, (half, size), 0)
     column = lax.broadcasted_iota(jnp.int32, (half, size), 1)
-    for slot, (grad, far) in enumerate(((grad_0, far_0), (grad_1, far_1))):
-        total[...] = grad[...]
+    for slot, extra in enumerate((extra_0, extra_1)):
+        total[...] = extra[2]
         for mode, other in enumerate((other_a, other_b)):
-            real, imag = to_sample(tab, far[mode, 0], far[mode, 1])
+            real, imag = to_sample(tab, extra[mode, 0], extra[mode, 1])
             pr, pi = other[0], other[1]
             total[0] += pr * real + pi * imag
             total[1] += pr * imag - pi * real
@@ -264,7 +264,7 @@
                     target[part, :, size:] += amount - near
 
 
-def diffuse_kernel(total_rows, above, tile, below, out):
+def diffuse_kernel(total_rows, outer, tile, inner, out):
     rows = tile.shape[1]
     columns = tile.shape[2]
     flat = own_diff() * lax.axis_size("obj") + lax.axis_index("obj")
@@ -273,7 +273,12 @@
     column = lax.broadcasted_iota(jnp.int32, (full, columns), 1)
     has_below = (row >= 0) & (row < total_rows - 1)
     has_right = column < columns - 1
-    now = [jnp.concatenate([above[p], tile[p], below[p]], axis=0) for p in range(2)]
+    first = lax.axis_index("obj") == 0
+    now = []
+    for p in range(2):
+        above = jnp.where(first, outer[p], inner[p])
+        below = jnp.where(first, inner[p], outer[p])
+        now.append(jnp.concatenate([above, tile[p], below], axis=0))
 
     def flux(axis, length, valid):
         step = [pltpu.roll(v, length - 1, axis) - v for v in now]
@@ -320,6 +325,7 @@
 
     both = shape(2, 2, size, size)
     patch = shape(2, size, size)
+    more = shape(3, 2, size, size)
     scratch = [
         pltpu.VMEM((2, size, size), F32),
         pltpu.VMEM((4, 2, size, size), F32),
@@ -327,13 +333,13 @@
         pltpu.VMEM((2, size // 2, size), F32),
     ]
     specs = [SMEM, SMEM] + [VMEM] * 7
-    grads, patch_0, far_0 = call(
+    grads, extra_0 = call(
         functools.partial(slot_kernel, 0, False),
-        [both, patch, both], specs, scratch, 24,
+        [both, more], specs, scratch, 24,
     )(offsets, counts, mine[0], theirs_0, probe_modes, other_a, other_b, amp, tab)
-    keep, send, patch_1, far_1 = call(
+    keep, send, extra_1 = call(
         functools.partial(slot_kernel, 1, True),
-        [patch, patch, patch, both], specs + [VMEM], scratch, 24,
+        [patch, patch, more], specs + [VMEM], scratch, 24,
     )(offsets, counts, mine[1], theirs_1, probe_modes, other_a, other_b, amp, tab, grads)
 
     summed = keep + lax.ppermute(send, "core", swap)
@@ -356,18 +362,22 @@
     own, spill = call(
         spread_kernel,
         [tile, tile],
-        [SMEM, SMEM] + [VMEM] * 7,
+        [SMEM, SMEM] + [VMEM] * 5,
         [pltpu.VMEM((2, size, size), F32)],
         16,
-    )(offsets, counts, other_a, other_b, tab, patch_0, far_0, patch_1, far_1)
+    )(offsets, counts, other_a, other_b, tab, extra_0, extra_1)
     arrived = shifted(spill, DIFF, n_diff, 1)
     raised = object_field + OBJECT_STEP * (own + arrived)
     flat = DIFF + ("obj",)
-    above = shifted(raised[:, tile_rows - HALO :], flat, n_diff * n_obj, 1)
-    below = shifted(raised[:, :HALO], flat, n_diff * n_obj, -1)
+    first = lax.axis_index("obj") == 0
+    top, low = raised[:, :HALO], raised[:, tile_rows - HALO :]
+    count = n_diff * n_obj
+    apart = [(i, j) for k in range(1, count - 1, 2) for i, j in ((k, k + 1), (k + 1, k))]
+    outer = lax.ppermute(jnp.where(first, top, low), flat, apart)
+    inner = lax.ppermute(jnp.where(first, low, top), "obj", swap)
     smooth = call(
         functools.partial(diffuse_kernel, total_rows), tile, [VMEM] * 3, ()
-    )(above, raised, below)
+    )(outer, raised, inner)
     return smooth, probe_out
 
 

time: 125 us -> 122 us (0.976)
  starting transfers between devices: 38.9 us -> 36.3 us
  local copies, waits for them, and re-layouts: 7.33 us -> 9.74 us
  waiting for transfers between devices: 53.1 us -> 51.7 us
    ppermute x4 -> x2, waiting for transfers between devices: 16.2 us -> 8.08 us  [shifted(): lax.ppermute(value, axes, [(i, i + steps) for i in range(count) if 0 <= i...]
    ppermute x0 -> x2, waiting for transfers between devices: none -> 7.23 us  [the longest x1 7.23 us: body(): outer = lax.ppermute(jnp.where(first, top, low), flat, apart)]
    ppermute x4 -> x2, starting transfers between devices: 12.7 us -> 6.77 us  [shifted(): lax.ppermute(value, axes, [(i, i + steps) for i in range(count) if 0 <= i...]
    ppermute x0 -> x2, starting transfers between devices: none -> 3.43 us  [the longest x1 1.92 us: body(): outer = lax.ppermute(jnp.where(first, top, low), flat, apart)]
    unnamed x34 -> x26, local copies, waits for them, and re-layouts: 5.31 us -> 7.68 us
    ppermute x1, waiting for transfers between devices: 5.35 us -> 3.36 us  [body(): theirs_0 = lax.ppermute(mine[0], 'obj', swap)]
    all_to_all x1, waiting for transfers between devices: 5.02 us -> 6.41 us  [body(): lax.all_to_all(jnp.broadcast_to(share[None], pieces.shape), 'chip', 0, 0)]
  transfers between devices with their start and end apart: 12 -> 12, of which waited for: 8 -> 8; matrix products, arithmetic and copies ran while one was open for 1% -> 0% of each run, Pallas kernels for 11% -> 11%
where the time goes in v2:
time: 122 us
  waiting for transfers between devices  51.7 us (42%)
  starting transfers between devices  36.3 us (30%)
  Pallas kernels  18.5 us (15%)
  local copies, waits for them, and re-layouts  9.74 us (8%)
  other arithmetic  4.48 us (4%)
    all_to_all x1, waiting for transfers between devices, body(): gathered = lax.all_to_all(pieces, 'chip', 0, 0)  16.3 us
    all_to_all x1, starting transfers between devices, body(): gathered = lax.all_to_all(pieces, 'chip', 0, 0)  11.3 us
    all_to_all x1, starting transfers between devices, body(): lax.all_to_all(jnp.broadcast_to(share[None], pieces.shape), 'chip', 0, 0)  9.07 us
    ppermute x1, waiting for transfers between devices, body(): other_a = lax.ppermute(mode, DIFF + ('obj',), probe_pairs(n_chip, n_obj))  8.35 us
    ppermute x2, waiting for transfers between devices, shifted(): lax.ppermute(value, axes, [(i, i + steps) for i in range(count) if 0 <= i...  8.08 us
    unnamed x26, local copies, waits for them, and re-layouts  7.68 us
    ppermute x1, waiting for transfers between devices, body(): outer = lax.ppermute(jnp.where(first, top, low), flat, apart)  7.23 us
    ppermute x2, starting transfers between devices, shifted(): lax.ppermute(value, axes, [(i, i + steps) for i in range(count) if 0 <= i...  6.77 us
  transfers between devices with their start and end apart: 12, of which 8 were waited for; matrix products, arithmetic and copies ran while one was open for 0% of the time, Pallas kernels for 11%

profile of v2, /device:TPU:128, one launch (start us, length us, event | category | flops | bytes accessed | tf_op | source)
XLA Modules:
  0.0 121.6 jit_solution(10464983853753890163)
XLA Ops:
  0.6 0.0 copy-start.11
  0.7 0.0 copy-start
  0.7 1.2 %dynamic-slice_bitcast_fusion = f32[2,256,256]{2,1,0:T(8,128)S(1)} fusion(f32[2,2,256,256]{3,2,1,0:T(8,128)} %own.5, s32[]{:T(128)S(6)} %select_n.29), kind=kLoop, calls=%fused_computation.2 | loop fusion | bytes 1048580 | tf_op jit(solution)/shard_map/jit(dynamic_index_in_dim)/squeeze | solution.py:315
  1.9 1.7 %collective-permute-start = (f32[2,256,256]{2,1,0:T(8,128)S(1)}, f32[2,256,256]{2,1,0:T(8,128)S(1)}, u32[]{:S(2)}, u32[]{:S(2)}) collective-permute-start(f32[2,256,256]{2,1,0:T(8,128)S(1)} %dynamic-slice_bitcast_fusion), channel_id=1, source_target_pairs={{0,1},{1,0},{2,7},{3,6},{4,5},{5,4},{6,3},{7,2},{8,9},{9,8},{10,15... | collective-permute-start | bytes 1572872 | tf_op jit(solution)/shard_map/ppermute | solution.py:316
  3.6 4.9 %collective-permute-start.2 = (f32[2,128,512]{2,1,0:T(8,128)}, f32[2,128,512]{2,1,0:T(8,128)S(1)}, u32[]{:S(2)}, u32[]{:S(2)}) collective-permute-start(f32[2,128,512]{2,1,0:T(8,128)} %own.3), channel_id=1, source_target_pairs={{2,0},{4,2},{6,4},{8,6},{10,8},{12,10},{14,12},{16,14},{18,16},{20... | collective-permute-start | bytes 1572872 | tf_op jit(solution)/shard_map/ppermute | solution.py:299
  8.4 8.4 %collective-permute-done.other_a = f32[2,256,256]{2,1,0:T(8,128)S(1)} collective-permute-done((f32[2,256,256]{2,1,0:T(8,128)S(1)}, f32[2,256,256]{2,1,0:T(8,128)S(1)}, u32[]{:S(2)}, u32[]{:S(2)}) %collective-permute-start) | collective-permute-done | bytes 524320 | tf_op jit(solution)/shard_map/ppermute | solution.py:316
  16.8 0.0 collective-permute-start.1
  16.8 0.0 collective-permute-done.2.following
  16.8 1.0 copy-done.2
  17.9 0.7 copy-done.10
  18.5 0.6 shard_map.86
  19.2 1.7 %collective-permute-start.3 = (f32[2,128,256]{2,1,0:T(8,128)S(1)}, f32[2,128,256]{2,1,0:T(8,128)S(1)}, u32[]{:S(2)}, u32[]{:S(2)}) collective-permute-start(f32[2,128,256]{2,1,0:T(8,128)S(1)} %get-tuple-element.11.mine), channel_id=1, source_target_pairs={{0,1},{1,0},{2,3},{3,2},{4,5},{5,4},{6,7},{7,6},{8,9},{9,8},{10,11... | collective-permute-start | bytes 786440 | tf_op jit(solution)/shard_map/ppermute | solution.py:323
  20.8 0.4 collective-permute-start.4
  21.3 1.0 copy-done.8
  22.3 0.9 copy-done.9
  23.3 0.9 shard_map.87.amp
  24.2 3.4 %collective-permute-done.3.theirs = f32[2,128,256]{2,1,0:T(8,128)S(1)} collective-permute-done((f32[2,128,256]{2,1,0:T(8,128)S(1)}, f32[2,128,256]{2,1,0:T(8,128)S(1)}, u32[]{:S(2)}, u32[]{:S(2)}) %collective-permute-start.3) | collective-permute-done | bytes 262176 | tf_op jit(solution)/shard_map/ppermute | solution.py:323
  27.5 0.0 collective-permute-done.1.other_b
  27.5 0.0 copy-done
  27.6 5.2 %shard_map.88 = (f32[2,2,256,256]{3,2,1,0:T(8,128)S(1)}, f32[3,2,256,256]{3,2,1,0:T(8,128)S(1)}) custom-call(s32[2,2]{1,0:T(2,128)S(1)} %copy-done.11, s32[128]{0:T(128)S(1)} %copy-done.12, f32[2,128,256]{2,1,0:T(8,128)S(1)} %get-tuple-element.11.mine, f32[2,128,256]{2,1,0:T(8,128)S(1)} %collective-permute-done.3.theirs, f32[2,2,256,256]{3,2,1,0:T(8,128)S(1)} %copy-done.1, ...), custom_call_target="tpu_custom_call" | custom-call | tf_op jit(solution)/shard_map/pallas_call | solution.py:336
  32.8 0.4 collective-permute-done.4.theirs
  33.2 5.3 %shard_map.89 = (f32[2,256,256]{2,1,0:T(8,128)S(1)}, f32[2,256,256]{2,1,0:T(8,128)S(1)}, f32[3,2,256,256]{3,2,1,0:T(8,128)S(1)}) custom-call(s32[2,2]{1,0:T(2,128)S(1)} %copy-done.11, s32[128]{0:T(128)S(1)} %copy-done.12, f32[2,128,256]{2,1,0:T(8,128)S(1)} %get-tuple-element.13.mine, f32[2,128,256]{2,1,0:T(8,128)S(1)} %collective-permute-done.4.theirs, ...), custom_call_target="tpu_custom_call" | custom-call | tf_op jit(solution)/shard_map/pallas_call | solution.py:340
  38.5 0.0 copy-done.4
  38.5 0.0 copy-start.6
  38.5 1.1 copy-done.6
  39.6 1.9 %collective-permute-start.8 = (f32[2,256,256]{2,1,0:T(8,128)S(1)}, f32[2,256,256]{2,1,0:T(8,128)S(1)}, u32[]{:S(2)}, u32[]{:S(2)}) collective-permute-start(f32[2,256,256]{2,1,0:T(8,128)S(1)} %get-tuple-element.19), channel_id=1, source_target_pairs={{0,2},{2,0},{1,3},{3,1},{4,6},{6,4},{5,7},{7,5},{8,10},{10,8},{9,1... | collective-permute-start | bytes 1572872 | tf_op jit(solution)/shard_map/ppermute | solution.py:345
  41.6 1.5 %collective-permute-done.8 = f32[2,256,256]{2,1,0:T(8,128)S(1)} collective-permute-done((f32[2,256,256]{2,1,0:T(8,128)S(1)}, f32[2,256,256]{2,1,0:T(8,128)S(1)}, u32[]{:S(2)}, u32[]{:S(2)}) %collective-permute-start.8) | collective-permute-done | bytes 524320 | tf_op jit(solution)/shard_map/ppermute | solution.py:345
  43.1 0.9 add.28
  44.0 11.3 %all-to-all-start = ((f32[64,8,256]{2,1,0:T(8,128)}), f32[64,8,256]{2,1,0:T(8,128)}, u32[]{:S(2)}, u32[]{:S(2)}) async-start(f32[64,8,256]{2,1,0:T(8,128)} %bitcast.10), calls=%async_computation | async-start | bytes 1048576 | tf_op jit(solution)/shard_map/all_to_all | solution.py:347
  55.3 16.3 %all-to-all-done = f32[64,8,256]{2,1,0:T(8,128)} async-done(((f32[64,8,256]{2,1,0:T(8,128)}), f32[64,8,256]{2,1,0:T(8,128)}, u32[]{:S(2)}, u32[]{:S(2)}) %all-to-all-start) | async-done | bytes 524320 | tf_op jit(solution)/shard_map/all_to_all | solution.py:347
  71.6 1.1 reduce_sum.9
  72.7 0.8 broadcast_in_dim.2
  73.5 9.1 %all-to-all-start.1 = ((f32[64,8,256]{2,1,0:T(8,128)}), f32[64,8,256]{2,1,0:T(8,128)}, u32[]{:S(2)}, u32[]{:S(2)}) async-start(f32[64,8,256]{2,1,0:T(8,128)} %broadcast_in_dim.2), calls=%async_computation.1 | async-start | bytes 1048576 | tf_op jit(solution)/shard_map/all_to_all | solution.py:354
  82.6 1.4 %copy-done.5 = f32[3,2,256,256]{3,2,1,0:T(8,128)S(1)} copy-done((f32[3,2,256,256]{3,2,1,0:T(8,128)S(1)}, f32[3,2,256,256]{3,2,1,0:T(8,128)}, u32[]{:S(2)}) %copy-start.5) | copy-done | bytes 1572888
  84.0 1.4 %copy-done.7 = f32[3,2,256,256]{3,2,1,0:T(8,128)S(1)} copy-done((f32[3,2,256,256]{3,2,1,0:T(8,128)S(1)}, f32[3,2,256,256]{3,2,1,0:T(8,128)}, u32[]{:S(2)}) %copy-start.7) | copy-done | bytes 1572888
  85.4 4.3 %shard_map.90 = (f32[2,128,512]{2,1,0:T(8,128)S(1)}, f32[2,128,512]{2,1,0:T(8,128)}) custom-call(s32[2,2]{1,0:T(2,128)S(1)} %copy-done.11, s32[128]{0:T(128)S(1)} %copy-done.12, f32[2,256,256]{2,1,0:T(8,128)S(1)} %collective-permute-done.other_a, f32[2,256,256]{2,1,0:T(8,128)S(1)} %collective-permute-done.1.other_b, bf16[8,256,256]{2,1,0:T(8,128)(2,1)S(1)} %copy-done, ...), custom_call_target="tpu_custom_call" | custom-call | tf_op jit(solution)/shard_map/pallas_call | solution.py:362
  89.7 1.9 %collective-permute-start.5 = (f32[2,128,512]{2,1,0:T(8,128)}, f32[2,128,512]{2,1,0:T(8,128)S(1)}, u32[]{:S(2)}, u32[]{:S(2)}) collective-permute-start(f32[2,128,512]{2,1,0:T(8,128)} %get-tuple-element.17), channel_id=1, source_target_pairs={{0,2},{2,4},{4,6},{6,8},{8,10},{10,12},{12,14},{14,16},{16,18},{18... | collective-permute-start | bytes 1572872 | tf_op jit(solution)/shard_map/ppermute | solution.py:299
  91.6 6.4 %all-to-all-done.1 = f32[64,8,256]{2,1,0:T(8,128)} async-done(((f32[64,8,256]{2,1,0:T(8,128)}), f32[64,8,256]{2,1,0:T(8,128)}, u32[]{:S(2)}, u32[]{:S(2)}) %all-to-all-start.1) | async-done | bytes 524320 | tf_op jit(solution)/shard_map/all_to_all | solution.py:354
  98.0 0.0 collective-permute-start.9
  98.0 8.1 %collective-permute-done.5 = f32[2,128,512]{2,1,0:T(8,128)S(1)} collective-permute-done((f32[2,128,512]{2,1,0:T(8,128)}, f32[2,128,512]{2,1,0:T(8,128)S(1)}, u32[]{:S(2)}, u32[]{:S(2)}) %collective-permute-start.5) | collective-permute-done | bytes 524320 | tf_op jit(solution)/shard_map/ppermute | solution.py:299
  106.1 0.2 multiply_add_fusion.tile
  106.3 1.9 %collective-permute-start.6 = (f32[2,8,512]{2,1,0:T(8,128)S(1)}, f32[2,8,512]{2,1,0:T(8,128)S(1)}, u32[]{:S(2)}, u32[]{:S(2)}) collective-permute-start(f32[2,8,512]{2,1,0:T(8,128)S(1)} %get-tuple-element.21), channel_id=1, source_target_pairs={{1,2},{2,1},{3,4},{4,3},{5,6},{6,5},{7,8},{8,7},{9,10},{10,9},{11,... | collective-permute-start | bytes 98312 | tf_op jit(solution)/shard_map/ppermute | solution.py:376
  108.2 1.5 %collective-permute-start.7 = (f32[2,8,512]{2,1,0:T(8,128)S(1)}, f32[2,8,512]{2,1,0:T(8,128)S(1)}, u32[]{:S(2)}, u32[]{:S(2)}) collective-permute-start(f32[2,8,512]{2,1,0:T(8,128)S(1)} %get-tuple-element.20), channel_id=1, source_target_pairs={{0,1},{1,0},{2,3},{3,2},{4,5},{5,4},{6,7},{7,6},{8,9},{9,8},{10,11... | collective-permute-start | bytes 98312 | tf_op jit(solution)/shard_map/ppermute | solution.py:377
  109.7 7.2 %collective-permute-done.6.outer = f32[2,8,512]{2,1,0:T(8,128)S(1)} collective-permute-done((f32[2,8,512]{2,1,0:T(8,128)S(1)}, f32[2,8,512]{2,1,0:T(8,128)S(1)}, u32[]{:S(2)}, u32[]{:S(2)}) %collective-permute-start.6) | collective-permute-done | bytes 32800 | tf_op jit(solution)/shard_map/ppermute | solution.py:376
  117.0 0.0 collective-permute-done.7.inner
  117.0 2.3 %shard_map.91 = f32[2,128,512]{2,1,0:T(8,128)} custom-call(f32[2,8,512]{2,1,0:T(8,128)S(1)} %collective-permute-done.6.outer, f32[2,128,512]{2,1,0:T(8,128)S(1)} %multiply_add_fusion.tile, f32[2,8,512]{2,1,0:T(8,128)S(1)} %collective-permute-done.7.inner), custom_call_target="tpu_custom_call" | custom-call | tf_op jit(solution)/shard_map/pallas_call | solution.py:378
  119.2 0.0 collective-permute-done.9
  119.2 2.3 %maximum_select_fusion = f32[2,2,256,256]{3,2,1,0:T(8,128)} fusion(f32[1,2,256,256]{3,2,1,0:T(8,128)S(1)} %bitcast.11, f32[1,2,256,256]{3,2,1,0:T(8,128)} %bitcast.4, pred[]{:T(512)S(6)} %eq.7), kind=kLoop, calls=%fused_computation | loop fusion | flops 786432 | bytes 2097153 | tf_op jit(solution)/shard_map/jit(_where)/select_n | solution.py:357
  (16 shorter events, 0.0 us)
Async XLA Ops:
  0.6 26.9 %copy-start.11 = (s32[2,2]{1,0:T(2,128)S(1)}, s32[2,2]{1,0:T(2,128)}, u32[]{:S(2)}) copy-start(s32[2,2]{1,0:T(2,128)} %offs.7) | copy-start | bytes 52
  0.6 26.9 %copy-start.12 = (s32[128]{0:T(128)S(1)}, s32[128]{0:T(128)}, u32[]{:S(2)}) copy-start(s32[128]{0:T(128)} %counts.5) | copy-start | bytes 1540
  0.7 26.9 %copy-start = (bf16[8,256,256]{2,1,0:T(8,128)(2,1)S(1)}, bf16[8,256,256]{2,1,0:T(8,128)(2,1)}, u32[]{:S(2)}) copy-start(bf16[8,256,256]{2,1,0:T(8,128)(2,1)} %constant.33.clone.tab) | copy-start | bytes 3145732
  0.7 26.9 %copy-start.1 = (f32[2,2,256,256]{3,2,1,0:T(8,128)S(1)}, f32[2,2,256,256]{3,2,1,0:T(8,128)}, u32[]{:S(2)}) copy-start(f32[2,2,256,256]{3,2,1,0:T(8,128)} %own.5) | copy-start | bytes 3145732
  1.9 14.9 %collective-permute-start = (f32[2,256,256]{2,1,0:T(8,128)S(1)}, f32[2,256,256]{2,1,0:T(8,128)S(1)}, u32[]{:S(2)}, u32[]{:S(2)}) collective-permute-start(f32[2,256,256]{2,1,0:T(8,128)S(1)} %dynamic-slice_bitcast_fusion), channel_id=1, source_target_pairs={{0,1},{1,0},{2,7},{3,6},{4,5},{5,4},{6,3},{7,2},{8,9},{9,8},{10,15... | collective-permute-start | bytes 1572872 | tf_op jit(solution)/shard_map/ppermute | solution.py:316
  3.6 13.2 %collective-permute-start.2 = (f32[2,128,512]{2,1,0:T(8,128)}, f32[2,128,512]{2,1,0:T(8,128)S(1)}, u32[]{:S(2)}, u32[]{:S(2)}) collective-permute-start(f32[2,128,512]{2,1,0:T(8,128)} %own.3), channel_id=1, source_target_pairs={{2,0},{4,2},{6,4},{8,6},{10,8},{12,10},{14,12},{16,14},{18,16},{20... | collective-permute-start | bytes 1572872 | tf_op jit(solution)/shard_map/ppermute | solution.py:299
  16.8 10.7 %collective-permute-start.1 = (f32[2,256,256]{2,1,0:T(8,128)S(1)}, f32[2,256,256]{2,1,0:T(8,128)S(1)}, u32[]{:S(2)}, u32[]{:S(2)}) collective-permute-start(f32[2,256,256]{2,1,0:T(8,128)S(1)} %collective-permute-done.other_a), channel_id=1, source_target_pairs={{0,2},{2,0},{1,3},{3,1},{4,6},{6,4},{5,7},{7,5},{8,10},{10,8},{9,1... | collective-permute-start | bytes 1572872 | tf_op jit(solution)/shard_map/ppermute | solution.py:317
  16.8 1.0 copy-start.2
  17.8 0.7 copy-start.10
  19.2 8.4 %collective-permute-start.3 = (f32[2,128,256]{2,1,0:T(8,128)S(1)}, f32[2,128,256]{2,1,0:T(8,128)S(1)}, u32[]{:S(2)}, u32[]{:S(2)}) collective-permute-start(f32[2,128,256]{2,1,0:T(8,128)S(1)} %get-tuple-element.11.mine), channel_id=1, source_target_pairs={{0,1},{1,0},{2,3},{3,2},{4,5},{5,4},{6,7},{7,6},{8,9},{9,8},{10,11... | collective-permute-start | bytes 786440 | tf_op jit(solution)/shard_map/ppermute | solution.py:323
  20.8 12.3 %collective-permute-start.4 = (f32[2,128,256]{2,1,0:T(8,128)S(1)}, f32[2,128,256]{2,1,0:T(8,128)S(1)}, u32[]{:S(2)}, u32[]{:S(2)}) collective-permute-start(f32[2,128,256]{2,1,0:T(8,128)S(1)} %get-tuple-element.13.mine), channel_id=1, source_target_pairs={{0,1},{1,0},{2,3},{3,2},{4,5},{5,4},{6,7},{7,6},{8,9},{9,8},{10,11... | collective-permute-start | bytes 786440 | tf_op jit(solution)/shard_map/ppermute | solution.py:324
  21.3 1.0 copy-start.8
  22.3 0.9 copy-start.9
  32.8 5.7 %copy-start.4 = (f32[3,2,256,256]{3,2,1,0:T(8,128)}, f32[3,2,256,256]{3,2,1,0:T(8,128)S(1)}, u32[]{:S(2)}) copy-start(f32[3,2,256,256]{3,2,1,0:T(8,128)S(1)} %get-tuple-element.12.extra_0) | copy-start | bytes 4718596
  38.5 1.1 copy-start.6
  39.6 3.5 %collective-permute-start.8 = (f32[2,256,256]{2,1,0:T(8,128)S(1)}, f32[2,256,256]{2,1,0:T(8,128)S(1)}, u32[]{:S(2)}, u32[]{:S(2)}) collective-permute-start(f32[2,256,256]{2,1,0:T(8,128)S(1)} %get-tuple-element.19), channel_id=1, source_target_pairs={{0,2},{2,0},{1,3},{3,1},{4,6},{6,4},{5,7},{7,5},{8,10},{10,8},{9,1... | collective-permute-start | bytes 1572872 | tf_op jit(solution)/shard_map/ppermute | solution.py:345
  44.0 27.6 %all-to-all-start = ((f32[64,8,256]{2,1,0:T(8,128)}), f32[64,8,256]{2,1,0:T(8,128)}, u32[]{:S(2)}, u32[]{:S(2)}) async-start(f32[64,8,256]{2,1,0:T(8,128)} %bitcast.10), calls=%async_computation | async-start | bytes 1048576 | tf_op jit(solution)/shard_map/all_to_all | solution.py:347
  73.5 24.5 %all-to-all-start.1 = ((f32[64,8,256]{2,1,0:T(8,128)}), f32[64,8,256]{2,1,0:T(8,128)}, u32[]{:S(2)}, u32[]{:S(2)}) async-start(f32[64,8,256]{2,1,0:T(8,128)} %broadcast_in_dim.2), calls=%async_computation.1 | async-start | bytes 1048576 | tf_op jit(solution)/shard_map/all_to_all | solution.py:354
  82.6 1.4 %copy-start.5 = (f32[3,2,256,256]{3,2,1,0:T(8,128)S(1)}, f32[3,2,256,256]{3,2,1,0:T(8,128)}, u32[]{:S(2)}) copy-start(f32[3,2,256,256]{3,2,1,0:T(8,128)} %copy-done.4) | copy-start | bytes 4718596
  84.0 1.4 %copy-start.7 = (f32[3,2,256,256]{3,2,1,0:T(8,128)S(1)}, f32[3,2,256,256]{3,2,1,0:T(8,128)}, u32[]{:S(2)}) copy-start(f32[3,2,256,256]{3,2,1,0:T(8,128)} %copy-done.6) | copy-start | bytes 4718596
  85.4 20.7 %copy-start.3 = (f32[2,128,512]{2,1,0:T(8,128)S(1)}, f32[2,128,512]{2,1,0:T(8,128)}, u32[]{:S(2)}) copy-start(f32[2,128,512]{2,1,0:T(8,128)} %own.3) | copy-start | bytes 1572868
  89.7 16.4 %collective-permute-start.5 = (f32[2,128,512]{2,1,0:T(8,128)}, f32[2,128,512]{2,1,0:T(8,128)S(1)}, u32[]{:S(2)}, u32[]{:S(2)}) collective-permute-start(f32[2,128,512]{2,1,0:T(8,128)} %get-tuple-element.17), channel_id=1, source_target_pairs={{0,2},{2,4},{4,6},{6,8},{8,10},{10,12},{12,14},{14,16},{16,18},{18... | collective-permute-start | bytes 1572872 | tf_op jit(solution)/shard_map/ppermute | solution.py:299
  98.0 21.2 %collective-permute-start.9 = (f32[2,256,256]{2,1,0:T(8,128)}, f32[2,256,256]{2,1,0:T(8,128)S(1)}, u32[]{:S(2)}, u32[]{:S(2)}) collective-permute-start(f32[2,256,256]{2,1,0:T(8,128)} %bitcast.5), channel_id=1, source_target_pairs={{0,2},{2,0},{1,3},{3,1},{4,6},{6,4},{5,7},{7,5},{8,10},{10,8},{9,1... | collective-permute-start | bytes 1572872 | tf_op jit(solution)/shard_map/ppermute | solution.py:356
  106.3 10.7 %collective-permute-start.6 = (f32[2,8,512]{2,1,0:T(8,128)S(1)}, f32[2,8,512]{2,1,0:T(8,128)S(1)}, u32[]{:S(2)}, u32[]{:S(2)}) collective-permute-start(f32[2,8,512]{2,1,0:T(8,128)S(1)} %get-tuple-element.21), channel_id=1, source_target_pairs={{1,2},{2,1},{3,4},{4,3},{5,6},{6,5},{7,8},{8,7},{9,10},{10,9},{11,... | collective-permute-start | bytes 98312 | tf_op jit(solution)/shard_map/ppermute | solution.py:376
  108.2 8.7 %collective-permute-start.7 = (f32[2,8,512]{2,1,0:T(8,128)S(1)}, f32[2,8,512]{2,1,0:T(8,128)S(1)}, u32[]{:S(2)}, u32[]{:S(2)}) collective-permute-start(f32[2,8,512]{2,1,0:T(8,128)S(1)} %get-tuple-element.20), channel_id=1, source_target_pairs={{0,1},{1,0},{2,3},{3,2},{4,5},{5,4},{6,7},{7,6},{8,9},{9,8},{10,11... | collective-permute-start | bytes 98312 | tf_op jit(solution)/shard_map/ppermute | solution.py:377

commit v3 on v2

--- a/solution.py
+++ b/solution.py
@@ -21,15 +21,18 @@
 DIFF = ("chip", "core")
 VMEM = pl.BlockSpec(memory_space=pltpu.VMEM)
 SMEM = pl.BlockSpec(memory_space=pltpu.SMEM)
-
-
-def call(kernel, out_shape, in_specs, scratch=(), mib=8):
+HBM = pl.BlockSpec(memory_space=pltpu.HBM)
+
+
+def call(kernel, out_shape, in_specs, scratch=(), mib=8, out_specs=None):
     single = not isinstance(out_shape, (tuple, list))
+    if out_specs is None:
+        out_specs = VMEM if single else [VMEM] * len(out_shape)
     return pl.pallas_call(
         kernel,
         out_shape=out_shape,
         in_specs=in_specs,
-        out_specs=VMEM if single else [VMEM] * len(out_shape),
+        out_specs=out_specs,
         scratch_shapes=list(scratch),
         compiler_params=pltpu.CompilerParams(vmem_limit_bytes=mib << 20),
         interpret=INTERPRET,
@@ -185,7 +188,7 @@
 
 def slot_kernel(slot, last, offs, counts, mine, theirs, own, other_a, other_b, amp, tab, *rest):
     if last:
-        before, grad_keep, grad_send, extra, field, far, grads, power = rest
+        before, grad_keep, grad_send, extra_out, field, far, grads, power, extra, sem = rest
     else:
         grads, extra, field, far, _, power = rest
     size = own.shape[-1]
@@ -229,9 +232,12 @@
         grads[mode, 0] = weight * (fr * real + fi * imag)
         grads[mode, 1] = weight * (fr * imag - fi * real)
     if last:
+        saved = pltpu.make_async_copy(extra, extra_out, sem)
+        saved.start()
         core = lax.axis_index("core")
         grad_keep[...] = before[core] + grads[core]
         grad_send[...] = before[1 - core] + grads[1 - core]
+        saved.wait()
 
 
 def spread_kernel(offs, counts, other_a, other_b, tab, extra_0, extra_1, own, spill, total):
@@ -264,6 +270,27 @@
                     target[part, :, size:] += amount - near
 
 
+def share_kernel(n_diff, gathered, start, out):
+    parts = [gathered[i] for i in range(8)]
+    for chip in range(8, gathered.shape[0]):
+        parts[chip % 8] += gathered[chip]
+    while len(parts) > 1:
+        parts = [a + b for a, b in zip(parts[::2], parts[1::2])]
+    share = start[...] + parts[0] / n_diff
+    for chip in range(gathered.shape[0]):
+        out[chip] = share
+
+
+def order_kernel(updated, remote, out, sems):
+    core = lax.axis_index("core")
+    mine = pltpu.make_async_copy(updated, out.at[core], sems.at[0])
+    other = pltpu.make_async_copy(remote, out.at[1 - core], sems.at[1])
+    mine.start()
+    other.start()
+    mine.wait()
+    other.wait()
+
+
 def diffuse_kernel(total_rows, outer, tile, inner, out):
     rows = tile.shape[1]
     columns = tile.shape[2]
@@ -339,24 +366,32 @@
     )(offsets, counts, mine[0], theirs_0, probe_modes, other_a, other_b, amp, tab)
     keep, send, extra_1 = call(
         functools.partial(slot_kernel, 1, True),
-        [patch, patch, more], specs + [VMEM], scratch, 24,
+        [patch, patch, pltpu.HBM(more.shape, F32)], specs + [VMEM],
+        scratch + [pltpu.VMEM(more.shape, F32), pltpu.SemaphoreType.DMA], 24,
+        [VMEM, VMEM, HBM],
     )(offsets, counts, mine[1], theirs_1, probe_modes, other_a, other_b, amp, tab, grads)
 
     summed = keep + lax.ppermute(send, "core", swap)
     pieces = summed.reshape(n_chip, 2 * size // n_chip, size)
     gathered = lax.all_to_all(pieces, "chip", 0, 0)
-    share = jnp.sum(gathered, axis=0)
     views = probe_modes.reshape(2, n_chip, 2 * size // n_chip, size)
     start = lax.dynamic_slice(
         views, (core, lax.axis_index("chip"), 0, 0), (1, 1) + views.shape[2:]
     )[0, 0]
-    share = start + share / n_diff
-    updated = lax.all_to_all(jnp.broadcast_to(share[None], pieces.shape), "chip", 0, 0)
+    share = call(
+        functools.partial(share_kernel, n_diff), shape(*pieces.shape), [VMEM] * 2
+    )(gathered, start)
+    updated = lax.all_to_all(share, "chip", 0, 0)
     updated = updated.reshape(2, size, size)
     remote = lax.ppermute(updated, "core", swap)
-    probe_out = jnp.where(
-        core == 0, jnp.stack([updated, remote]), jnp.stack([remote, updated])
-    )
+    probe_out = call(
+        order_kernel,
+        pltpu.HBM((2, 2, size, size), F32),
+        [VMEM, VMEM],
+        [pltpu.SemaphoreType.DMA((2,))],
+        4,
+        HBM,
+    )(updated, remote)
 
     tile = shape(2, tile_rows, columns)
     own, spill = call(

time: 122 us -> 123 us (level)
  Pallas kernels: 18.5 us -> 22.6 us
  other arithmetic: 4.48 us -> 2.08 us
    pallas_call x1 -> x3, Pallas kernels: 5.31 us -> 9.37 us  [the longest x1 6.47 us: body(): call(functools.partial(slot_kernel, 1, True), [patch, patch, pltpu.HBM(mo...]
    select_n x1 -> x0, other arithmetic: 2.34 us -> none  [body(): jnp.where(core == 0, jnp.stack([updated, remote]), jnp.stack([remote, upd...]
  transfers between devices with their start and end apart: 12 -> 12, of which waited for: 8 -> 8; matrix products, arithmetic and copies ran while one was open for 0% -> 1% of each run, Pallas kernels for 11% -> 11%
where the time goes in v3:
time: 123 us; the launch traced here: 122 us
  waiting for transfers between devices  51.7 us (42%)
  starting transfers between devices  36.3 us (30%)
  Pallas kernels  22.6 us (18%)
  local copies, waits for them, and re-layouts  8.58 us (7%)
  other arithmetic  2.08 us (2%)
    all_to_all x1, waiting for transfers between devices, body(): gathered = lax.all_to_all(pieces, 'chip', 0, 0)  16.3 us
    all_to_all x1, starting transfers between devices, body(): gathered = lax.all_to_all(pieces, 'chip', 0, 0)  11.3 us
    all_to_all x1, starting transfers between devices, body(): updated = lax.all_to_all(share, 'chip', 0, 0)  9.07 us
    ppermute x2, waiting for transfers between devices, shifted(): lax.ppermute(value, axes, [(i, i + steps) for i in range(count) if 0 <= i...  8.78 us
    ppermute x1, waiting for transfers between devices, body(): other_a = lax.ppermute(mode, DIFF + ('obj',), probe_pairs(n_chip, n_obj))  8.35 us
    unnamed x26, local copies, waits for them, and re-layouts  7.34 us
    ppermute x1, waiting for transfers between devices, body(): outer = lax.ppermute(jnp.where(first, top, low), flat, apart)  7.24 us
    ppermute x2, starting transfers between devices, shifted(): lax.ppermute(value, axes, [(i, i + steps) for i in range(count) if 0 <= i...  6.77 us
  transfers between devices with their start and end apart: 12, of which 8 were waited for; matrix products, arithmetic and copies ran while one was open for 1% of the time, Pallas kernels for 11%

profile of v3, /device:TPU:128, one launch (start us, length us, event | category | flops | bytes accessed | tf_op | source)
XLA Modules:
  0.0 122.2 jit_solution(3582374705152950981)
XLA Ops:
  0.6 0.0 copy-start.11
  0.7 0.0 copy-start
  0.7 1.2 %dynamic-slice_bitcast_fusion = f32[2,256,256]{2,1,0:T(8,128)S(1)} fusion(f32[2,2,256,256]{3,2,1,0:T(8,128)} %own.5, s32[]{:T(128)S(6)} %select_n.21), kind=kLoop, calls=%fused_computation.1 | loop fusion | bytes 1048580 | tf_op jit(solution)/shard_map/jit(dynamic_index_in_dim)/squeeze | solution.py:342
  1.9 1.7 %collective-permute-start = (f32[2,256,256]{2,1,0:T(8,128)S(1)}, f32[2,256,256]{2,1,0:T(8,128)S(1)}, u32[]{:S(2)}, u32[]{:S(2)}) collective-permute-start(f32[2,256,256]{2,1,0:T(8,128)S(1)} %dynamic-slice_bitcast_fusion), channel_id=1, source_target_pairs={{0,1},{1,0},{2,7},{3,6},{4,5},{5,4},{6,3},{7,2},{8,9},{9,8},{10,15... | collective-permute-start | bytes 1572872 | tf_op jit(solution)/shard_map/ppermute | solution.py:343
  3.6 4.9 %collective-permute-start.2 = (f32[2,128,512]{2,1,0:T(8,128)}, f32[2,128,512]{2,1,0:T(8,128)S(1)}, u32[]{:S(2)}, u32[]{:S(2)}) collective-permute-start(f32[2,128,512]{2,1,0:T(8,128)} %own.3), channel_id=1, source_target_pairs={{2,0},{4,2},{6,4},{8,6},{10,8},{12,10},{14,12},{16,14},{18,16},{20... | collective-permute-start | bytes 1572872 | tf_op jit(solution)/shard_map/ppermute | solution.py:326
  8.4 8.4 %collective-permute-done.other_a = f32[2,256,256]{2,1,0:T(8,128)S(1)} collective-permute-done((f32[2,256,256]{2,1,0:T(8,128)S(1)}, f32[2,256,256]{2,1,0:T(8,128)S(1)}, u32[]{:S(2)}, u32[]{:S(2)}) %collective-permute-start) | collective-permute-done | bytes 524320 | tf_op jit(solution)/shard_map/ppermute | solution.py:343
  16.8 0.0 collective-permute-start.1
  16.8 0.0 collective-permute-done.2.following
  16.8 1.0 copy-done.2
  17.9 0.7 copy-done.10
  18.5 0.6 shard_map.86
  19.2 1.7 %collective-permute-start.3 = (f32[2,128,256]{2,1,0:T(8,128)S(1)}, f32[2,128,256]{2,1,0:T(8,128)S(1)}, u32[]{:S(2)}, u32[]{:S(2)}) collective-permute-start(f32[2,128,256]{2,1,0:T(8,128)S(1)} %get-tuple-element.11.mine), channel_id=1, source_target_pairs={{0,1},{1,0},{2,3},{3,2},{4,5},{5,4},{6,7},{7,6},{8,9},{9,8},{10,11... | collective-permute-start | bytes 786440 | tf_op jit(solution)/shard_map/ppermute | solution.py:350
  20.8 0.4 collective-permute-start.4
  21.3 1.0 copy-done.7
  22.3 0.9 copy-done.9
  23.3 0.9 shard_map.87.amp
  24.2 3.4 %collective-permute-done.3.theirs = f32[2,128,256]{2,1,0:T(8,128)S(1)} collective-permute-done((f32[2,128,256]{2,1,0:T(8,128)S(1)}, f32[2,128,256]{2,1,0:T(8,128)S(1)}, u32[]{:S(2)}, u32[]{:S(2)}) %collective-permute-start.3) | collective-permute-done | bytes 262176 | tf_op jit(solution)/shard_map/ppermute | solution.py:350
  27.5 0.0 collective-permute-done.1.other_b
  27.5 0.0 copy-done
  27.6 5.2 %shard_map.88 = (f32[2,2,256,256]{3,2,1,0:T(8,128)S(1)}, f32[3,2,256,256]{3,2,1,0:T(8,128)S(1)}) custom-call(s32[2,2]{1,0:T(2,128)S(1)} %copy-done.11, s32[128]{0:T(128)S(1)} %copy-done.12, f32[2,128,256]{2,1,0:T(8,128)S(1)} %get-tuple-element.11.mine, f32[2,128,256]{2,1,0:T(8,128)S(1)} %collective-permute-done.3.theirs, f32[2,2,256,256]{3,2,1,0:T(8,128)S(1)} %copy-done.1, ...), custom_call_target="tpu_custom_call" | custom-call | tf_op jit(solution)/shard_map/pallas_call | solution.py:363
  32.8 0.4 collective-permute-done.4.theirs
  33.2 6.5 %shard_map.89 = (f32[2,256,256]{2,1,0:T(8,128)S(1)}, f32[2,256,256]{2,1,0:T(8,128)S(1)}, f32[3,2,256,256]{3,2,1,0:T(8,128)}) custom-call(s32[2,2]{1,0:T(2,128)S(1)} %copy-done.11, s32[128]{0:T(128)S(1)} %copy-done.12, f32[2,128,256]{2,1,0:T(8,128)S(1)} %get-tuple-element.13.mine, f32[2,128,256]{2,1,0:T(8,128)S(1)} %collective-permute-done.4.theirs, ...), custom_call_target="tpu_custom_call" | custom-call | tf_op jit(solution)/shard_map/pallas_call | solution.py:367
  39.6 0.0 copy-done.4
  39.6 2.0 %collective-permute-start.8 = (f32[2,256,256]{2,1,0:T(8,128)S(1)}, f32[2,256,256]{2,1,0:T(8,128)S(1)}, u32[]{:S(2)}, u32[]{:S(2)}) collective-permute-start(f32[2,256,256]{2,1,0:T(8,128)S(1)} %get-tuple-element.19), channel_id=1, source_target_pairs={{0,2},{2,0},{1,3},{3,1},{4,6},{6,4},{5,7},{7,5},{8,10},{10,8},{9,1... | collective-permute-start | bytes 1572872 | tf_op jit(solution)/shard_map/ppermute | solution.py:374
  41.7 1.5 %collective-permute-done.8 = f32[2,256,256]{2,1,0:T(8,128)S(1)} collective-permute-done((f32[2,256,256]{2,1,0:T(8,128)S(1)}, f32[2,256,256]{2,1,0:T(8,128)S(1)}, u32[]{:S(2)}, u32[]{:S(2)}) %collective-permute-start.8) | collective-permute-done | bytes 524320 | tf_op jit(solution)/shard_map/ppermute | solution.py:374
  43.2 0.9 add.20
  44.1 11.3 %all-to-all-start = ((f32[64,8,256]{2,1,0:T(8,128)}), f32[64,8,256]{2,1,0:T(8,128)}, u32[]{:S(2)}, u32[]{:S(2)}) async-start(f32[64,8,256]{2,1,0:T(8,128)} %bitcast.10), calls=%async_computation | async-start | bytes 1048576 | tf_op jit(solution)/shard_map/all_to_all | solution.py:376
  55.4 16.3 %all-to-all-done.gathered = f32[64,8,256]{2,1,0:T(8,128)} async-done(((f32[64,8,256]{2,1,0:T(8,128)}), f32[64,8,256]{2,1,0:T(8,128)}, u32[]{:S(2)}, u32[]{:S(2)}) %all-to-all-start) | async-done | bytes 524320 | tf_op jit(solution)/shard_map/all_to_all | solution.py:376
  71.7 1.9 %shard_map.92 = f32[64,8,256]{2,1,0:T(8,128)} custom-call(f32[64,8,256]{2,1,0:T(8,128)} %all-to-all-done.gathered, f32[8,256]{1,0:T(8,128)S(1)} %dynamic-slice_bitcast_fusion.1.start), custom_call_target="tpu_custom_call" | custom-call | tf_op jit(solution)/shard_map/pallas_call | solution.py:381
  73.6 9.1 %all-to-all-start.1 = ((f32[64,8,256]{2,1,0:T(8,128)}), f32[64,8,256]{2,1,0:T(8,128)S(1)}, u32[]{:S(2)}, u32[]{:S(2)}) async-start(f32[64,8,256]{2,1,0:T(8,128)} %shard_map.92), calls=%async_computation.1 | async-start | bytes 1048576 | tf_op jit(solution)/shard_map/all_to_all | solution.py:384
  82.7 0.0 copy-start.5
  82.7 1.4 %copy-done.5 = f32[3,2,256,256]{3,2,1,0:T(8,128)S(1)} copy-done((f32[3,2,256,256]{3,2,1,0:T(8,128)S(1)}, f32[3,2,256,256]{3,2,1,0:T(8,128)}, u32[]{:S(2)}) %copy-start.5) | copy-done | bytes 1572888
  84.1 1.4 %copy-done.6 = f32[3,2,256,256]{3,2,1,0:T(8,128)S(1)} copy-done((f32[3,2,256,256]{3,2,1,0:T(8,128)S(1)}, f32[3,2,256,256]{3,2,1,0:T(8,128)}, u32[]{:S(2)}) %copy-start.6) | copy-done | bytes 1572888
  85.5 4.3 %shard_map.90 = (f32[2,128,512]{2,1,0:T(8,128)S(1)}, f32[2,128,512]{2,1,0:T(8,128)}) custom-call(s32[2,2]{1,0:T(2,128)S(1)} %copy-done.11, s32[128]{0:T(128)S(1)} %copy-done.12, f32[2,256,256]{2,1,0:T(8,128)S(1)} %collective-permute-done.other_a, f32[2,256,256]{2,1,0:T(8,128)S(1)} %collective-permute-done.1.other_b, bf16[8,256,256]{2,1,0:T(8,128)(2,1)S(1)} %copy-done, ...), custom_call_target="tpu_custom_call" | custom-call | tf_op jit(solution)/shard_map/pallas_call | solution.py:397
  89.8 0.8 copy-done.8
  90.5 1.9 %collective-permute-start.5 = (f32[2,128,512]{2,1,0:T(8,128)}, f32[2,128,512]{2,1,0:T(8,128)S(1)}, u32[]{:S(2)}, u32[]{:S(2)}) collective-permute-start(f32[2,128,512]{2,1,0:T(8,128)} %get-tuple-element.17), channel_id=1, source_target_pairs={{0,2},{2,4},{4,6},{6,8},{8,10},{10,12},{12,14},{14,16},{16,18},{18... | collective-permute-start | bytes 1572872 | tf_op jit(solution)/shard_map/ppermute | solution.py:326
  92.5 5.7 %all-to-all-done.1 = f32[64,8,256]{2,1,0:T(8,128)S(1)} async-done(((f32[64,8,256]{2,1,0:T(8,128)}), f32[64,8,256]{2,1,0:T(8,128)S(1)}, u32[]{:S(2)}, u32[]{:S(2)}) %all-to-all-start.1) | async-done | bytes 524320 | tf_op jit(solution)/shard_map/all_to_all | solution.py:384
  98.2 0.0 collective-permute-start.9
  98.2 8.8 %collective-permute-done.5 = f32[2,128,512]{2,1,0:T(8,128)S(1)} collective-permute-done((f32[2,128,512]{2,1,0:T(8,128)}, f32[2,128,512]{2,1,0:T(8,128)S(1)}, u32[]{:S(2)}, u32[]{:S(2)}) %collective-permute-start.5) | collective-permute-done | bytes 524320 | tf_op jit(solution)/shard_map/ppermute | solution.py:326
  107.0 0.0 copy-done.3
  107.0 1.2 multiply_add_fusion.tile
  108.2 1.9 %collective-permute-start.6 = (f32[2,8,512]{2,1,0:T(8,128)S(1)}, f32[2,8,512]{2,1,0:T(8,128)S(1)}, u32[]{:S(2)}, u32[]{:S(2)}) collective-permute-start(f32[2,8,512]{2,1,0:T(8,128)S(1)} %get-tuple-element.21), channel_id=1, source_target_pairs={{1,2},{2,1},{3,4},{4,3},{5,6},{6,5},{7,8},{8,7},{9,10},{10,9},{11,... | collective-permute-start | bytes 98312 | tf_op jit(solution)/shard_map/ppermute | solution.py:411
  110.1 1.5 %collective-permute-start.7 = (f32[2,8,512]{2,1,0:T(8,128)S(1)}, f32[2,8,512]{2,1,0:T(8,128)S(1)}, u32[]{:S(2)}, u32[]{:S(2)}) collective-permute-start(f32[2,8,512]{2,1,0:T(8,128)S(1)} %get-tuple-element.20), channel_id=1, source_target_pairs={{0,1},{1,0},{2,3},{3,2},{4,5},{5,4},{6,7},{7,6},{8,9},{9,8},{10,11... | collective-permute-start | bytes 98312 | tf_op jit(solution)/shard_map/ppermute | solution.py:412
  111.6 7.2 %collective-permute-done.6.outer = f32[2,8,512]{2,1,0:T(8,128)S(1)} collective-permute-done((f32[2,8,512]{2,1,0:T(8,128)S(1)}, f32[2,8,512]{2,1,0:T(8,128)S(1)}, u32[]{:S(2)}, u32[]{:S(2)}) %collective-permute-start.6) | collective-permute-done | bytes 32800 | tf_op jit(solution)/shard_map/ppermute | solution.py:411
  118.9 0.0 collective-permute-done.7.inner
  118.9 2.2 %shard_map.91 = f32[2,128,512]{2,1,0:T(8,128)} custom-call(f32[2,8,512]{2,1,0:T(8,128)S(1)} %collective-permute-done.6.outer, f32[2,128,512]{2,1,0:T(8,128)S(1)} %multiply_add_fusion.tile, f32[2,8,512]{2,1,0:T(8,128)S(1)} %collective-permute-done.7.inner), custom_call_target="tpu_custom_call" | custom-call | tf_op jit(solution)/shard_map/pallas_call | solution.py:413
  121.1 0.0 collective-permute-done.9.remote
  121.1 1.0 shard_map.93
  (15 shorter events, 0.0 us)
Async XLA Ops:
  0.6 26.9 %copy-start.11 = (s32[2,2]{1,0:T(2,128)S(1)}, s32[2,2]{1,0:T(2,128)}, u32[]{:S(2)}) copy-start(s32[2,2]{1,0:T(2,128)} %offs.7) | copy-start | bytes 52
  0.6 26.9 %copy-start.12 = (s32[128]{0:T(128)S(1)}, s32[128]{0:T(128)}, u32[]{:S(2)}) copy-start(s32[128]{0:T(128)} %counts.5) | copy-start | bytes 1540
  0.7 26.9 %copy-start = (bf16[8,256,256]{2,1,0:T(8,128)(2,1)S(1)}, bf16[8,256,256]{2,1,0:T(8,128)(2,1)}, u32[]{:S(2)}) copy-start(bf16[8,256,256]{2,1,0:T(8,128)(2,1)} %constant.28.clone.tab) | copy-start | bytes 3145732
  0.7 26.9 %copy-start.1 = (f32[2,2,256,256]{3,2,1,0:T(8,128)S(1)}, f32[2,2,256,256]{3,2,1,0:T(8,128)}, u32[]{:S(2)}) copy-start(f32[2,2,256,256]{3,2,1,0:T(8,128)} %own.5) | copy-start | bytes 3145732
  1.9 14.9 %collective-permute-start = (f32[2,256,256]{2,1,0:T(8,128)S(1)}, f32[2,256,256]{2,1,0:T(8,128)S(1)}, u32[]{:S(2)}, u32[]{:S(2)}) collective-permute-start(f32[2,256,256]{2,1,0:T(8,128)S(1)} %dynamic-slice_bitcast_fusion), channel_id=1, source_target_pairs={{0,1},{1,0},{2,7},{3,6},{4,5},{5,4},{6,3},{7,2},{8,9},{9,8},{10,15... | collective-permute-start | bytes 1572872 | tf_op jit(solution)/shard_map/ppermute | solution.py:343
  3.6 13.2 %collective-permute-start.2 = (f32[2,128,512]{2,1,0:T(8,128)}, f32[2,128,512]{2,1,0:T(8,128)S(1)}, u32[]{:S(2)}, u32[]{:S(2)}) collective-permute-start(f32[2,128,512]{2,1,0:T(8,128)} %own.3), channel_id=1, source_target_pairs={{2,0},{4,2},{6,4},{8,6},{10,8},{12,10},{14,12},{16,14},{18,16},{20... | collective-permute-start | bytes 1572872 | tf_op jit(solution)/shard_map/ppermute | solution.py:326
  16.8 10.7 %collective-permute-start.1 = (f32[2,256,256]{2,1,0:T(8,128)S(1)}, f32[2,256,256]{2,1,0:T(8,128)S(1)}, u32[]{:S(2)}, u32[]{:S(2)}) collective-permute-start(f32[2,256,256]{2,1,0:T(8,128)S(1)} %collective-permute-done.other_a), channel_id=1, source_target_pairs={{0,2},{2,0},{1,3},{3,1},{4,6},{6,4},{5,7},{7,5},{8,10},{10,8},{9,1... | collective-permute-start | bytes 1572872 | tf_op jit(solution)/shard_map/ppermute | solution.py:344
  16.8 1.0 copy-start.2
  17.8 0.7 copy-start.10
  19.2 8.4 %collective-permute-start.3 = (f32[2,128,256]{2,1,0:T(8,128)S(1)}, f32[2,128,256]{2,1,0:T(8,128)S(1)}, u32[]{:S(2)}, u32[]{:S(2)}) collective-permute-start(f32[2,128,256]{2,1,0:T(8,128)S(1)} %get-tuple-element.11.mine), channel_id=1, source_target_pairs={{0,1},{1,0},{2,3},{3,2},{4,5},{5,4},{6,7},{7,6},{8,9},{9,8},{10,11... | collective-permute-start | bytes 786440 | tf_op jit(solution)/shard_map/ppermute | solution.py:350
  20.8 12.3 %collective-permute-start.4 = (f32[2,128,256]{2,1,0:T(8,128)S(1)}, f32[2,128,256]{2,1,0:T(8,128)S(1)}, u32[]{:S(2)}, u32[]{:S(2)}) collective-permute-start(f32[2,128,256]{2,1,0:T(8,128)S(1)} %get-tuple-element.13.mine), channel_id=1, source_target_pairs={{0,1},{1,0},{2,3},{3,2},{4,5},{5,4},{6,7},{7,6},{8,9},{9,8},{10,11... | collective-permute-start | bytes 786440 | tf_op jit(solution)/shard_map/ppermute | solution.py:351
  21.3 1.0 copy-start.7
  22.3 0.9 copy-start.9
  32.8 6.9 %copy-start.4 = (f32[3,2,256,256]{3,2,1,0:T(8,128)}, f32[3,2,256,256]{3,2,1,0:T(8,128)S(1)}, u32[]{:S(2)}) copy-start(f32[3,2,256,256]{3,2,1,0:T(8,128)S(1)} %get-tuple-element.12.extra_0) | copy-start | bytes 4718596
  39.6 3.6 %collective-permute-start.8 = (f32[2,256,256]{2,1,0:T(8,128)S(1)}, f32[2,256,256]{2,1,0:T(8,128)S(1)}, u32[]{:S(2)}, u32[]{:S(2)}) collective-permute-start(f32[2,256,256]{2,1,0:T(8,128)S(1)} %get-tuple-element.19), channel_id=1, source_target_pairs={{0,2},{2,0},{1,3},{3,1},{4,6},{6,4},{5,7},{7,5},{8,10},{10,8},{9,1... | collective-permute-start | bytes 1572872 | tf_op jit(solution)/shard_map/ppermute | solution.py:374
  44.1 27.6 %all-to-all-start = ((f32[64,8,256]{2,1,0:T(8,128)}), f32[64,8,256]{2,1,0:T(8,128)}, u32[]{:S(2)}, u32[]{:S(2)}) async-start(f32[64,8,256]{2,1,0:T(8,128)} %bitcast.10), calls=%async_computation | async-start | bytes 1048576 | tf_op jit(solution)/shard_map/all_to_all | solution.py:376
  73.6 24.6 %all-to-all-start.1 = ((f32[64,8,256]{2,1,0:T(8,128)}), f32[64,8,256]{2,1,0:T(8,128)S(1)}, u32[]{:S(2)}, u32[]{:S(2)}) async-start(f32[64,8,256]{2,1,0:T(8,128)} %shard_map.92), calls=%async_computation.1 | async-start | bytes 1048576 | tf_op jit(solution)/shard_map/all_to_all | solution.py:384
  82.7 1.4 %copy-start.5 = (f32[3,2,256,256]{3,2,1,0:T(8,128)S(1)}, f32[3,2,256,256]{3,2,1,0:T(8,128)}, u32[]{:S(2)}) copy-start(f32[3,2,256,256]{3,2,1,0:T(8,128)} %copy-done.4) | copy-start | bytes 4718596
  84.1 1.4 %copy-start.6 = (f32[3,2,256,256]{3,2,1,0:T(8,128)S(1)}, f32[3,2,256,256]{3,2,1,0:T(8,128)}, u32[]{:S(2)}) copy-start(f32[3,2,256,256]{3,2,1,0:T(8,128)} %get-tuple-element.15.extra_1) | copy-start | bytes 4718596
  85.5 21.5 %copy-start.3 = (f32[2,128,512]{2,1,0:T(8,128)S(1)}, f32[2,128,512]{2,1,0:T(8,128)}, u32[]{:S(2)}) copy-start(f32[2,128,512]{2,1,0:T(8,128)} %own.3) | copy-start | bytes 1572868
  89.8 0.8 copy-start.8
  90.5 16.4 %collective-permute-start.5 = (f32[2,128,512]{2,1,0:T(8,128)}, f32[2,128,512]{2,1,0:T(8,128)S(1)}, u32[]{:S(2)}, u32[]{:S(2)}) collective-permute-start(f32[2,128,512]{2,1,0:T(8,128)} %get-tuple-element.17), channel_id=1, source_target_pairs={{0,2},{2,4},{4,6},{6,8},{8,10},{10,12},{12,14},{14,16},{16,18},{18... | collective-permute-start | bytes 1572872 | tf_op jit(solution)/shard_map/ppermute | solution.py:326
  98.2 22.9 %collective-permute-start.9 = (f32[2,256,256]{2,1,0:T(8,128)S(1)}, f32[2,256,256]{2,1,0:T(8,128)S(1)}, u32[]{:S(2)}, u32[]{:S(2)}) collective-permute-start(f32[2,256,256]{2,1,0:T(8,128)S(1)} %bitcast.8), channel_id=1, source_target_pairs={{0,2},{2,0},{1,3},{3,1},{4,6},{6,4},{5,7},{7,5},{8,10},{10,8},{9,1... | collective-permute-start | bytes 1572872 | tf_op jit(solution)/shard_map/ppermute | solution.py:386
  108.2 10.7 %collective-permute-start.6 = (f32[2,8,512]{2,1,0:T(8,128)S(1)}, f32[2,8,512]{2,1,0:T(8,128)S(1)}, u32[]{:S(2)}, u32[]{:S(2)}) collective-permute-start(f32[2,8,512]{2,1,0:T(8,128)S(1)} %get-tuple-element.21), channel_id=1, source_target_pairs={{1,2},{2,1},{3,4},{4,3},{5,6},{6,5},{7,8},{8,7},{9,10},{10,9},{11,... | collective-permute-start | bytes 98312 | tf_op jit(solution)/shard_map/ppermute | solution.py:411
  110.1 8.7 %collective-permute-start.7 = (f32[2,8,512]{2,1,0:T(8,128)S(1)}, f32[2,8,512]{2,1,0:T(8,128)S(1)}, u32[]{:S(2)}, u32[]{:S(2)}) collective-permute-start(f32[2,8,512]{2,1,0:T(8,128)S(1)} %get-tuple-element.20), channel_id=1, source_target_pairs={{0,1},{1,0},{2,3},{3,2},{4,5},{5,4},{6,7},{7,6},{8,9},{9,8},{10,11... | collective-permute-start | bytes 98312 | tf_op jit(solution)/shard_map/ppermute | solution.py:412
